TPU v7x, 32 devices: a whole 2x2x4 slice. The times are simulated.
32 devices in a mesh: parts: 2 (over y), blk: 4 (over z), win: 2 (over x), bin: 2 (over core).
Axes of the slice: x: 2, y: 2, z: 4, core: 2. Of those that a mesh axis runs over, the one named last changes fastest.
Arguments:
- raw_counts: bfloat16 [2400, 8, 640], P(('win', 'bin'), ('parts', 'blk')), parts along dimension 1, may hold values from -6 to 6
- seg_valid: int32 [4, 512], P(('win', 'bin'), ('parts', 'blk')), parts along dimension 1, may hold values 0 or 1
Outputs:
- pair_stacks: float32 [2, 8, 2, 320, 4096], P(None, ('parts', 'blk'), None, ('win', 'bin')), parts along dimension 1
There are 2 independent parts, one for each index of `parts`. A program takes and returns all parts, laid end to end along the dimension named above; each array names one. Nothing has to cross between parts.
All inputs are finite; a program needn't handle non-finite values. No bound on the sum of `seg_valid` on one device may be relied on, other than what follows from the above.
Results may differ from a plain program's by a relative error of at most 0.006.
Values may be sent and summed in bfloat16 or wider, within the bound.
No kernel may reach another device: no remote copies, remote signals or barrier semaphores. Data moves between devices by JAX's collectives and lax.ppermute only.
A program may use at most 64 MiB of HBM per device.

v0:
```python
import math

import jax
import jax.numpy as jnp
from jax import lax
from jax.sharding import PartitionSpec as P

SB = 64
LSEG = 600
NF = 320
DECIM = 10
TAPS = 64
SMOOTH = 33
ROUNDS = 2
HIST = 7


epsilon = 1e-06


def shifted(value, axis, steps):
    count = lax.axis_size(axis)
    first, last = (max(0, -steps), min(count, count - steps))
    return lax.ppermute(value, axis, [(source, source + steps) for source in range(first, last)])


def from_behind(block, axis, distance):
    devices = range(lax.axis_size(axis))
    route = [((i - distance) % len(devices), i) for i in devices]
    return lax.ppermute(block, axis, route)


def filter_coeffs():
    position = jnp.arange(TAPS, dtype=jnp.int32).astype(jnp.float32)
    centre = 0.5 * (TAPS - 1)
    cutoff = 0.4 / DECIM
    shaped = jnp.sinc(2.0 * cutoff * (position - centre))
    window = 0.54 - 0.46 * jnp.cos(2.0 * math.pi * position / (TAPS - 1))
    return 2.0 * cutoff * shaped * window


def polyphase():
    coeffs = filter_coeffs()
    delays = (
        DECIM * jnp.arange(HIST + 1, dtype=jnp.int32)[:, None]
        - jnp.arange(DECIM, dtype=jnp.int32)[None, :]
    )
    matches = delays[:, :, None] == jnp.arange(TAPS, dtype=jnp.int32)[None, None, :]
    return jnp.sum(jnp.where(matches, coeffs[None, None, :], 0.0), axis=2)


def fourier_table():
    row_index = jnp.arange(2 * NF, dtype=jnp.int32)
    frequency = row_index // 2 + 1
    component = row_index % 2
    position = jnp.arange(LSEG, dtype=jnp.int32)
    phase_step = frequency[:, None] * position[None, :] % (2 * LSEG)
    radians = phase_step.astype(jnp.float32) * (math.pi / LSEG)
    return jnp.where(component[:, None] == 0, jnp.cos(radians), -jnp.sin(radians)).astype(
        jnp.bfloat16
    )


def smoother():
    row_index = jnp.arange(NF, dtype=jnp.int32)
    first_bin = jnp.clip(row_index - SMOOTH // 2, 0, NF - SMOOTH)
    columns = jnp.arange(NF, dtype=jnp.int32)[None, :]
    inside = (columns >= first_bin[:, None]) & (columns < first_bin[:, None] + SMOOTH)
    return inside.astype(jnp.float32)


def decimate(samples, history):
    row_count = samples.shape[0]
    extended = jnp.concatenate([history, samples], 0).astype(jnp.float32)
    extended = extended.reshape(row_count + HIST, DECIM, SB)
    weights = polyphase()
    running = jnp.zeros((row_count, SB), jnp.float32)
    for offset_back in range(HIST + 1):
        window_rows = extended[HIST - offset_back : HIST - offset_back + row_count]
        running = running + jnp.sum(window_rows * weights[offset_back][None, :, None], axis=1)
    return running.astype(jnp.bfloat16)


def whiten(decimated, validity):
    segments = decimated.shape[0] // LSEG
    framed = decimated.reshape(segments, LSEG, SB)
    spectra = jnp.einsum("kn,sni->ski", fourier_table(), framed, preferred_element_type=jnp.float32)
    paired = spectra.reshape(segments, NF, 2, SB)
    energy = jnp.sum(paired * paired, axis=2)
    smoothed = jnp.einsum("fg,sgi->sfi", smoother(), energy, precision=lax.Precision.HIGHEST) / (
        2.0 * SMOOTH
    )
    scaling = validity.astype(jnp.float32)[:, None, :] / jnp.sqrt(smoothed + epsilon)
    return (paired * scaling[:, :, None, :]).astype(jnp.bfloat16).reshape(segments, NF, 2 * SB)


def cross_block(home_spec, away_spec, seg_total):
    products = jnp.einsum("sfa,sfb->fab", home_spec, away_spec, preferred_element_type=jnp.float32)
    bin_count = home_spec.shape[1]
    quarters = products.reshape(bin_count, 2, SB, 2, SB)
    real_part = quarters[:, 0, :, 0, :] + quarters[:, 1, :, 1, :]
    imag_part = quarters[:, 1, :, 0, :] - quarters[:, 0, :, 1, :]
    return jnp.stack([real_part, imag_part], 0).reshape(2, bin_count, SB * SB) / seg_total


def per_device(raw_counts, seg_valid):
    samples = raw_counts[:, 0, :]
    row_count = samples.shape[0]
    history = shifted(samples[row_count - HIST :], ("win", "bin"), 1)
    spectra = whiten(decimate(samples, history), seg_valid)
    gathered = lax.all_to_all(spectra, ("win", "bin"), split_axis=1, concat_axis=0, tiled=True)
    seg_total = gathered.shape[0]
    stacks = []
    for offset in range(1, ROUNDS + 1):
        partner = from_behind(gathered, "blk", offset)
        stacks.append(cross_block(gathered, partner, seg_total))
    return jnp.stack(stacks, 0)[:, None]


def solution(mesh):
    in_specs = (P(("win", "bin"), ("parts", "blk"), None), P(("win", "bin"), ("parts", "blk")))
    out_specs = P(None, ("parts", "blk"), None, ("win", "bin"), None)
    return jax.shard_map(
        per_device, mesh=mesh, in_specs=in_specs, out_specs=out_specs, check_vma=False
    )
```

profile of v0, /device:TPU:0, one launch (start us, length us, event | category | flops | bytes accessed | tf_op | source)
XLA Modules:
  0.0 99.0 jit_solution(5481962043775870666)
XLA Ops:
  0.0 1.8 %copy.54 = bf16[600,1,640]{0,2,1:T(8,128)(2,1)S(1)} copy(bf16[600,1,640]{2,0,1:T(8,128)(2,1)} %param.2) | data formatting | bytes 1536000 | tf_op args[0]
  1.8 0.1 slice_bitcast_fusion
  2.0 2.4 %collective-permute-start = (bf16[7,640]{0,1:T(8,128)(2,1)S(1)}, bf16[7,640]{0,1:T(8,128)(2,1)S(1)}, u32[]{:S(2)}, u32[]{:S(2)}) collective-permute-start(bf16[7,640]{0,1:T(8,128)(2,1)S(1)} %slice_bitcast_fusion), channel_id=1, source_target_pairs={{0,1},{1,2},{2,3},{4,5},{5,6},{6,7},{8,9},{9,10},{10,11},{12,13},{... | collective-permute-start | bytes 26888 | tf_op jit(solution)/shard_map/ppermute | solution.py:24
  4.5 0.2 select_reduce_fusion
  4.6 0.3 slice_reduce_fusion.6
  5.0 0.4 collective-permute-done
  5.4 0.4 maximum_convert_fusion
  5.7 7.3 %fusion.38 = (f32[600,640]{0,1:T(8,128)}, f32[600,640]{0,1:T(8,128)}, f32[600,640]{0,1:T(8,128)}, f32[600,640]{0,1:T(8,128)}, f32[600,640]{0,1:T(8,128)}, /*inde...) fusion(f32[607,640]{0,1:T(8,128)S(1)} %maximum_convert_fusion), kind=kLoop, calls=%fused_computation.92 | loop fusion | bytes 24576000 | tf_op jit(solution)/shard_map/slice | solution.py:79
  13.0 2.4 %multiply_reduce_fusion.6 = (f32[600,64]{0,1:T(8,128)S(1)}, f32[600,64]{0,1:T(8,128)S(1)}) fusion(f32[600,10,64]{0,2,1:T(8,128)} %bitcast.59, f32[10]{0:T(128)S(1)} %get-tuple-element.5, f32[600,10,64]{0,2,1:T(8,128)} %bitcast.60, f32[10]{0:T(128)S(1)} %get-tuple-element.12), kind=kLoop, calls=%fused_computation.20 | loop fusion | flops 1459200 | bytes 3379280 | tf_op jit(solution)/shard_map/reduce_sum | solution.py:80
  15.5 0.5 copy-done.4
  15.9 0.3 multiply_reduce_fusion
  16.3 1.1 %copy-done.1 = f32[600,640]{0,1:T(8,128)S(1)} copy-done((f32[600,640]{0,1:T(8,128)S(1)}, f32[600,640]{0,1:T(8,128)}, u32[]{:S(2)}) %copy-start.1) | copy-done | bytes 1536024
  17.4 0.5 copy-done.2
  17.9 0.3 multiply_reduce_fusion.2
  18.2 1.1 %copy-done = f32[600,640]{0,1:T(8,128)S(1)} copy-done((f32[600,640]{0,1:T(8,128)S(1)}, f32[600,640]{0,1:T(8,128)}, u32[]{:S(2)}) %copy-start) | copy-done | bytes 1536024
  19.3 0.3 multiply_reduce_fusion.4
  19.7 7.1 %fusion.39 = (f32[1,640,64]{1,2,0:T(8,128)S(1)}, f32[1,640,64]{1,2,0:T(8,128)S(1)}) fusion(s32[640]{0:T(1024)S(1)} %fusion.20, pred[640]{0:T(1024)(128)(4,1)S(1)} %fusion.18, f32[600,64]{0,1:T(8,128)S(1)} %get-tuple-element.27, f32[600,64]{0,1:T(8,128)S(1)} %get-tuple-element.28, f32[600,64]{0,1:T(8,128)S(1)} %get-tuple-element.29, ...), kind=kOutput, calls=%fused_computation.93 | convolution fusion | flops 54108160 | bytes 1559680 | tf_op jit(solution)/shard_map/kn,sni->ski/dot_general | solution.py:87
  26.7 0.2 copy.57
  26.9 0.4 reduce_sum.99
  27.3 0.6 fusion.9
  27.9 0.3 copy.58
  28.2 0.2 copy.56
  28.4 0.1 reshape.373
  28.5 0.1 copy.81
  28.7 0.5 broadcast.262
  29.2 1.1 %reduce.18 = bf16[320,128]{1,0:T(8,128)(2,1)S(1)} reduce(bf16[320,1,128]{2,1,0:T(2,128)(2,1)S(1)} %bitcast.67, bf16[]{:T(256)} %broadcast.262), dimensions={1}, to_apply=%bitcast.46.reduce_sub_computation | reduce | bytes 163842
  30.3 11.5 %all_to_all.12 = bf16[4,2,5120]{2,1,0:T(2,128)(2,1)S(1)} all-to-all(bf16[4,2,5120]{2,1,0:T(2,128)(2,1)S(1)} %reshape.384), channel_id=1, replica_groups=mesh['parts'=2,'blk'=4,'win'=2,'bin'=2] {'win','bin'}, dimensions={0} | all-to-all | bytes 163840 | tf_op jit(solution)/shard_map/all_to_all | solution.py:111
  41.8 0.1 reshape.385
  41.9 0.7 copy.61
  42.6 2.6 %collective-permute-start.2 = (bf16[4,80,128]{2,0,1:T(4,128)(2,1)}, bf16[4,80,128]{2,0,1:T(4,128)(2,1)S(1)}, u32[]{:S(2)}, u32[]{:S(2)}) collective-permute-start(bf16[4,80,128]{2,0,1:T(4,128)(2,1)} %copy.61), channel_id=1, source_target_pairs={{8,0},{12,4},{0,8},{4,12},{9,1},{13,5},{1,9},{5,13},{10,2},{14,6},... | collective-permute-start | bytes 245768 | tf_op jit(solution)/shard_map/ppermute | solution.py:30
  45.2 1.6 %collective-permute-start.1 = (bf16[4,80,128]{2,0,1:T(4,128)(2,1)}, bf16[4,80,128]{2,0,1:T(4,128)(2,1)}, u32[]{:S(2)}, u32[]{:S(2)}) collective-permute-start(bf16[4,80,128]{2,0,1:T(4,128)(2,1)} %copy.61), channel_id=1, source_target_pairs={{12,0},{0,4},{4,8},{8,12},{13,1},{1,5},{5,9},{9,13},{14,2},{2,6},{... | collective-permute-start | bytes 245768 | tf_op jit(solution)/shard_map/ppermute | solution.py:30
  46.7 3.7 %collective-permute-done.2 = bf16[4,80,128]{2,0,1:T(4,128)(2,1)S(1)} collective-permute-done((bf16[4,80,128]{2,0,1:T(4,128)(2,1)}, bf16[4,80,128]{2,0,1:T(4,128)(2,1)S(1)}, u32[]{:S(2)}, u32[]{:S(2)}) %collective-permute-start.2) | collective-permute-done | bytes 81952 | tf_op jit(solution)/shard_map/ppermute | solution.py:30
  50.4 3.3 %fusion.34 = f32[80,128,128]{2,1,0:T(8,128)} fusion(bf16[4,80,128]{2,0,1:T(4,128)(2,1)S(1)} %collective-permute-done.2, bf16[4,80,128]{2,1,0:T(8,128)(2,1)S(1)} %bitcast.64), kind=kOutput, calls=%fused_computation.88 | convolution fusion | flops 10485760 | bytes 5406720 | tf_op jit(solution)/shard_map/sfa,sfb->fab/dot_general | solution.py:98
  53.6 8.0 %copy.67 = f32[80,128,128]{0,2,1:T(8,128)} copy(f32[80,128,128]{2,1,0:T(8,128)} %fusion.34) | data formatting | bytes 10485760 | tf_op jit(solution)/shard_map/sfa,sfb->fab/dot_general | solution.py:98
  61.6 6.0 %slice_add_fusion = (f32[80,1,64,1,64]{0,4,3,2,1:T(8,128)}, f32[80,1,64,1,64]{0,4,3,2,1:T(8,128)S(1)}) fusion(f32[80,2,64,2,64]{0,4,3,2,1:T(8,128)} %bitcast.47), kind=kLoop, calls=%fused_computation.5 | loop fusion | flops 655360 | bytes 7864320 | tf_op jit(solution)/shard_map/add | solution.py:101
  67.6 1.9 %copy.73 = f32[1,1,80,4096]{3,2,1,0:T(8,128)S(1)} copy(f32[1,1,80,4096]{2,3,1,0:T(8,128)} %bitcast.51) | data formatting | bytes 2621440 | tf_op jit(solution)/shard_map/stack | solution.py:103
  69.5 1.7 %copy.74 = f32[1,1,80,4096]{3,2,1,0:T(8,128)} copy(f32[1,1,80,4096]{2,3,1,0:T(8,128)S(1)} %bitcast.49) | data formatting | bytes 2621440 | tf_op jit(solution)/shard_map/stack | solution.py:103
  71.2 0.0 collective-permute-done.1
  71.2 4.1 %fusion.36 = f32[80,128,128]{2,1,0:T(8,128)} fusion(bf16[4,80,128]{2,0,1:T(4,128)(2,1)} %collective-permute-done.1, bf16[4,80,128]{2,1,0:T(8,128)(2,1)S(1)} %bitcast.65), kind=kOutput, calls=%fused_computation.90 | convolution fusion | flops 10485760 | bytes 5406720 | tf_op jit(solution)/shard_map/sfa,sfb->fab/dot_general | solution.py:98
  75.3 8.0 %copy.62 = f32[80,128,128]{0,2,1:T(8,128)} copy(f32[80,128,128]{2,1,0:T(8,128)} %fusion.36) | data formatting | bytes 10485760 | tf_op jit(solution)/shard_map/sfa,sfb->fab/dot_general | solution.py:98
  83.3 6.0 %slice_add_fusion.1 = (f32[80,1,64,1,64]{0,4,3,2,1:T(8,128)}, f32[80,1,64,1,64]{0,4,3,2,1:T(8,128)S(1)}) fusion(f32[80,2,64,2,64]{0,4,3,2,1:T(8,128)} %bitcast.48), kind=kLoop, calls=%fused_computation.7 | loop fusion | flops 655360 | bytes 7864320 | tf_op jit(solution)/shard_map/add | solution.py:101
  89.2 2.8 %copy.71 = f32[1,1,80,4096]{3,2,1,0:T(8,128)} copy(f32[1,1,80,4096]{2,3,1,0:T(8,128)} %bitcast.52) | data formatting | bytes 2621440 | tf_op jit(solution)/shard_map/stack | solution.py:103
  92.0 1.6 %copy.72 = f32[1,1,80,4096]{3,2,1,0:T(8,128)} copy(f32[1,1,80,4096]{2,3,1,0:T(8,128)S(1)} %bitcast.50) | data formatting | bytes 2621440 | tf_op jit(solution)/shard_map/stack | solution.py:103
  93.6 1.7 %maximum_multiply_fusion.1 = f32[1,2,80,4096]{3,2,1,0:T(8,128)S(1)} fusion(f32[1,1,80,4096]{3,2,1,0:T(8,128)} %copy.74, f32[1,1,80,4096]{3,2,1,0:T(8,128)S(1)} %copy.73), kind=kLoop, calls=%fused_computation.2 | loop fusion | flops 1310720 | bytes 5242880 | tf_op jit(solution)/shard_map/div | solution.py:103
  95.3 0.0 copy-done.5
  95.4 0.4 copy-done.6
  95.7 0.3 maximum_multiply_fusion
  96.0 3.0 %maximum_bitcast_fusion = f32[2,1,2,80,4096]{4,3,2,1,0:T(8,128)} fusion(f32[1,2,80,4096]{3,2,1,0:T(8,128)S(1)} %maximum_multiply_fusion.1, f32[1,2,80,4096]{3,2,1,0:T(8,128)S(1)} %maximum_multiply_fusion), kind=kLoop, calls=%fused_computation | loop fusion | flops 1310720 | bytes 10485760 | tf_op jit(solution)/shard_map/broadcast_in_dim | solution.py:117
  (21 shorter events, 0.2 us)
Async XLA Ops:
  0.0 4.4 %copy-start.7 = (s32[1,64]{1,0:T(1,128)S(1)}, s32[1,64]{1,0:T(1,128)}, u32[]{:S(2)}) copy-start(s32[1,64]{1,0:T(1,128)} %param.3) | copy-start | bytes 772
  2.0 3.4 %collective-permute-start = (bf16[7,640]{0,1:T(8,128)(2,1)S(1)}, bf16[7,640]{0,1:T(8,128)(2,1)S(1)}, u32[]{:S(2)}, u32[]{:S(2)}) collective-permute-start(bf16[7,640]{0,1:T(8,128)(2,1)S(1)} %slice_bitcast_fusion), channel_id=1, source_target_pairs={{0,1},{1,2},{2,3},{4,5},{5,6},{6,7},{8,9},{9,10},{10,11},{12,13},{... | collective-permute-start | bytes 26888 | tf_op jit(solution)/shard_map/ppermute | solution.py:24
  13.0 2.4 %copy-start.3 = (f32[600,640]{0,1:T(8,128)S(1)}, f32[600,640]{0,1:T(8,128)}, u32[]{:S(2)}) copy-start(f32[600,640]{0,1:T(8,128)} %get-tuple-element.18) | copy-start | bytes 4608004
  13.0 2.9 %copy-start.4 = (f32[600,640]{0,1:T(8,128)S(1)}, f32[600,640]{0,1:T(8,128)}, u32[]{:S(2)}) copy-start(f32[600,640]{0,1:T(8,128)} %get-tuple-element.19) | copy-start | bytes 4608004
  15.9 1.4 %copy-start.1 = (f32[600,640]{0,1:T(8,128)S(1)}, f32[600,640]{0,1:T(8,128)}, u32[]{:S(2)}) copy-start(f32[600,640]{0,1:T(8,128)} %get-tuple-element.20) | copy-start | bytes 4608004
  15.9 1.9 %copy-start.2 = (f32[600,640]{0,1:T(8,128)S(1)}, f32[600,640]{0,1:T(8,128)}, u32[]{:S(2)}) copy-start(f32[600,640]{0,1:T(8,128)} %get-tuple-element.21) | copy-start | bytes 4608004
  17.9 1.4 %copy-start = (f32[600,640]{0,1:T(8,128)S(1)}, f32[600,640]{0,1:T(8,128)}, u32[]{:S(2)}) copy-start(f32[600,640]{0,1:T(8,128)} %get-tuple-element.23) | copy-start | bytes 4608004
  42.6 7.8 %collective-permute-start.2 = (bf16[4,80,128]{2,0,1:T(4,128)(2,1)}, bf16[4,80,128]{2,0,1:T(4,128)(2,1)S(1)}, u32[]{:S(2)}, u32[]{:S(2)}) collective-permute-start(bf16[4,80,128]{2,0,1:T(4,128)(2,1)} %copy.61), channel_id=1, source_target_pairs={{8,0},{12,4},{0,8},{4,12},{9,1},{13,5},{1,9},{5,13},{10,2},{14,6},... | collective-permute-start | bytes 245768 | tf_op jit(solution)/shard_map/ppermute | solution.py:30
  45.2 26.0 %collective-permute-start.1 = (bf16[4,80,128]{2,0,1:T(4,128)(2,1)}, bf16[4,80,128]{2,0,1:T(4,128)(2,1)}, u32[]{:S(2)}, u32[]{:S(2)}) collective-permute-start(bf16[4,80,128]{2,0,1:T(4,128)(2,1)} %copy.61), channel_id=1, source_target_pairs={{12,0},{0,4},{4,8},{8,12},{13,1},{1,5},{5,9},{9,13},{14,2},{2,6},{... | collective-permute-start | bytes 245768 | tf_op jit(solution)/shard_map/ppermute | solution.py:30
  93.6 1.7 %copy-start.5 = (f32[1,1,80,4096]{3,2,1,0:T(8,128)S(1)}, f32[1,1,80,4096]{3,2,1,0:T(8,128)}, u32[]{:S(2)}) copy-start(f32[1,1,80,4096]{3,2,1,0:T(8,128)} %copy.71) | copy-start | bytes 3932164
  93.6 2.1 %copy-start.6 = (f32[1,1,80,4096]{3,2,1,0:T(8,128)S(1)}, f32[1,1,80,4096]{3,2,1,0:T(8,128)}, u32[]{:S(2)}) copy-start(f32[1,1,80,4096]{3,2,1,0:T(8,128)} %copy.72) | copy-start | bytes 3932164
where the time goes:
time: 99.6 us; the launch traced here: 99 us
  local copies, waits for them, and re-layouts  39.3 us (39%)
  other arithmetic  22.3 us (22%)
  matrix products  15.1 us (15%)
  blocking collectives  11.5 us (12%)
  starting transfers between devices  6.57 us (7%)
  waiting for transfers between devices  4.08 us (4%)
    dot_general x2, local copies, waits for them, and re-layouts, cross_block(): jnp.einsum('sfa,sfb->fab', home_spec, away_spec, preferred_element_type=j...  15.9 us
    add x2, other arithmetic, cross_block(): real_part = quarters[:, 0, :, 0, :] + quarters[:, 1, :, 1, :]  11.9 us
    all_to_all x1, blocking collectives, per_device(): lax.all_to_all(spectra, ('win', 'bin'), split_axis=1, concat_axis=0, tile...  11.5 us
    another operation x4, local copies, waits for them, and re-layouts, cross_block(): jnp.stack([real_part, imag_part], 0).reshape(2, bin_count, SB * SB)  7.98 us
    dot_general x2, matrix products, cross_block(): jnp.einsum('sfa,sfb->fab', home_spec, away_spec, preferred_element_type=j...  7.41 us
    slice x1, local copies, waits for them, and re-layouts, decimate(): window_rows = extended[HIST - offset_back:HIST - offset_back + row_count]  7.31 us
    dot_general x1, matrix products, whiten(): jnp.einsum('kn,sni->ski', fourier_table(), framed, preferred_element_type...  7.09 us
    unnamed x21, local copies, waits for them, and re-layouts  6.05 us
  transfers between devices with their start and end apart: 3, of which 2 were waited for; matrix products, arithmetic and copies ran while one was open for 22% of the time, Pallas kernels for 0%

commit v1 on v0

v1 whole, which is shorter than its diff:
```python
import functools
import math

import jax
import jax.numpy as jnp
import numpy as np
from jax import lax
from jax.experimental import pallas as pl
from jax.experimental.pallas import tpu as pltpu
from jax.sharding import PartitionSpec as P

SB = 64
LSEG = 600
NF = 320
DECIM = 10
TAPS = 64
SMOOTH = 33
ROUNDS = 2
HIST = 7

EPSILON = 1e-06
LANES = 128
SUB = 8
HALF = 304
PACKED = HALF + 16
BF16 = jnp.bfloat16
F32 = jnp.float32


def filter_coeffs():
    position = np.arange(TAPS, dtype=np.float64)
    centre = 0.5 * (TAPS - 1)
    cutoff = 0.4 / DECIM
    shaped = np.sinc(2.0 * cutoff * (position - centre))
    window = 0.54 - 0.46 * np.cos(2.0 * math.pi * position / (TAPS - 1))
    return 2.0 * cutoff * shaped * window


def tap_matrix():
    coeffs = filter_coeffs()
    weights = np.zeros((DECIM, HIST + 1))
    for p in range(DECIM):
        for o in range(HIST + 1):
            t = DECIM * o - p
            if 0 <= t < TAPS:
                weights[p, o] = coeffs[t]
    full = np.kron(weights, np.eye(SB)).astype(np.float32)
    high = full.astype(BF16)
    low = (full - high.astype(np.float32)).astype(BF16)
    return high, low


def window_of(first, count):
    width = count + SMOOTH - 1
    start = min(max(first - SMOOTH // 2, 0), NF - width)
    own = list(range(first, first + count))
    return own, [f for f in range(start, start + width) if f not in set(own)]


def tables(chunks):
    count = NF // chunks
    position = np.arange(2 * HALF)
    transforms, smoothers = [], []
    for chunk in range(chunks):
        own, others = window_of(chunk * count, count)
        rows = [(f, c) for g in range(0, count, SUB) for c in range(2) for f in own[g : g + SUB]]
        rows += [(f, c) for c in range(2) for f in others]
        bins = np.array([f for f, _ in rows])
        comps = np.array([c for _, c in rows])
        radians = ((bins[:, None] + 1) * position[None, :] % (2 * LSEG)) * (math.pi / LSEG)
        table = np.where(comps[:, None] == 0, np.cos(radians), -np.sin(radians))
        transforms.append(np.where(position[None, :] < LSEG, table, 0.0).astype(BF16))
        low = np.clip(bins[: 2 * count] - SMOOTH // 2, 0, NF - SMOOTH)
        inside = (bins[None, :] >= low[:, None]) & (bins[None, :] < low[:, None] + SMOOTH)
        smoothers.append(inside.astype(BF16))
    return np.stack(transforms), np.stack(smoothers)


def low_lanes(shape):
    return lax.broadcasted_iota(jnp.int32, shape, len(shape) - 1) % LANES < SB


def swap(value):
    return pltpu.roll(value, SB, 1)


def decimate_kernel(x_ref, valid_ref, high_ref, low_ref, out_ref, y_ref, e_ref):
    rows = x_ref.shape[0]
    x = x_ref[...]
    y_ref[0:16, :] = jnp.zeros((16, y_ref.shape[1]), F32)
    y_ref[16 + rows :, :] = jnp.zeros((y_ref.shape[0] - 16 - rows, y_ref.shape[1]), F32)
    y_ref[16 : 16 + rows, :] = jnp.dot(x, high_ref[...], preferred_element_type=F32) + jnp.dot(
        x, low_ref[...], preferred_element_type=F32
    )
    total = y_ref[8 : 8 + 616, 0:LANES]
    for j in range(1, (HIST + 1) // 2):
        total = total + y_ref[8 - 2 * j : 8 - 2 * j + 616, j * LANES : (j + 1) * LANES]
    e_ref[...] = total
    first = e_ref[8 : 8 + HALF, :] + swap(e_ref[7 : 7 + HALF, :])
    second = swap(e_ref[8 + HALF : 8 + 2 * HALF, :]) + e_ref[7 + HALF : 7 + 2 * HALF, :]
    value = jnp.where(low_lanes((HALF, LANES)), first, second)
    rounded = value.astype(BF16)
    out_ref[0:HALF, :] = rounded
    rest = value - rounded.astype(F32)
    ends = jnp.where(low_lanes((SUB, LANES)), rest[0:SUB], rest[HALF - SUB : HALF])
    valid = jnp.broadcast_to(valid_ref[...], (SUB, LANES))
    out_ref[HALF:PACKED, :] = jnp.concatenate([ends, valid], 0).astype(BF16)


def whiten_kernel(sizes, *refs):
    n_win, n_bin = sizes
    count = n_win * n_bin
    parts, (table_ref, smooth_ref, out_ref, q_ref) = refs[:count], refs[count:]
    my_win, my_bin = lax.axis_index("win"), lax.axis_index("bin")
    lanes8 = low_lanes((SUB, LANES))
    heads, tails, valids = [], [], []
    for part in parts:
        extra = part[HALF:PACKED, :].astype(F32)
        heads.append(part[0:16, :].astype(F32)[0:SUB] + extra[0:SUB])
        tails.append(swap(part[HALF - 16 : HALF, :].astype(F32)[SUB:] + extra[0:SUB]))
        valids.append(extra[SUB : SUB + 1])
    starts = []
    for d in range(n_win):
        for e in range(n_bin):
            win = lax.rem(my_win - d + n_win, n_win)
            core = lax.rem(my_bin - e + n_bin, n_bin)
            after = (e + 1) % n_bin
            same = tails[d * n_bin + after]
            other = tails[(d + 1) % n_win * n_bin + after]
            first = core == 0
            use_same = jnp.where(first, 0.0, 1.0).astype(F32)
            use_other = jnp.where(jnp.logical_and(first, win != 0), 1.0, 0.0).astype(F32)
            starts.append(heads[d * n_bin + e] + same * use_same + other * use_other)
    lanes = low_lanes((HALF, LANES))
    scales = []
    for q in range(count // 2):
        a = parts[2 * q][0:HALF, :].astype(F32)
        b = parts[2 * q + 1][0:HALF, :].astype(F32)
        column = slice(q * LANES, (q + 1) * LANES)
        early = jnp.where(lanes, a, swap(b))
        late = jnp.where(lanes, swap(a), b)
        begin = jnp.where(lanes8, starts[2 * q], swap(starts[2 * q + 1]))
        q_ref[0:HALF, column] = jnp.concatenate([begin, early[SUB:]], 0).astype(BF16)
        q_ref[HALF:, column] = late.astype(BF16)
        scales.append(jnp.where(low_lanes((1, LANES)), valids[2 * q], valids[2 * q + 1]))
    valid = jnp.concatenate(scales, 1)
    spectra = jnp.dot(table_ref[...], q_ref[...], preferred_element_type=F32)
    square = spectra * spectra
    square_high = square.astype(BF16)
    square_low = (square - square_high.astype(F32)).astype(BF16)
    smooth = smooth_ref[...]
    energy = jnp.dot(smooth, square_high, preferred_element_type=F32) + jnp.dot(
        smooth, square_low, preferred_element_type=F32
    )
    scale = valid * lax.rsqrt(energy * (1.0 / (2.0 * SMOOTH)) + EPSILON)
    out_ref[...] = (spectra[0 : out_ref.shape[0]] * scale).astype(BF16)


def spread(tile):
    low = low_lanes((SUB, LANES))
    zero = jnp.zeros((SUB, LANES), F32)
    tiles = []
    for q in range(tile.shape[1] // LANES):
        x = tile[:, q * LANES : (q + 1) * LANES]
        r = swap(x)
        tiles.append(
            [jnp.where(low, x, zero), jnp.where(low, zero, r), jnp.where(low, r, zero), jnp.where(low, zero, x)]
        )
    return tiles


def home_kernel(home_ref, out_ref):
    rows, depth = out_ref.shape[1], out_ref.shape[2]
    row = lax.broadcasted_iota(jnp.int32, (rows, LANES), 0)
    lane = lax.broadcasted_iota(jnp.int32, (rows, LANES), 1)
    pick = jnp.where(lane % SB == 2 * (row // SUB) + lane // SB, 1.0, 0.0).astype(BF16)
    row = lax.broadcasted_iota(jnp.int32, (rows, depth), 0)
    lane = lax.broadcasted_iota(jnp.int32, (rows, depth), 1)
    diagonal = row % SUB == lane % SUB
    for g in range(out_ref.shape[0]):
        values = home_ref[16 * g : 16 * g + 16, :].astype(F32)
        real, imag = spread(values[0:SUB]), spread(values[SUB:])
        stack = []
        for q in range(len(real)):
            stack += real[q] + imag[q]
        block = jnp.concatenate(stack, 0).astype(BF16)
        turned = lax.dot_general(pick, block, (((1,), (1,)), ((), ())), preferred_element_type=F32)
        out_ref[g] = jnp.where(diagonal, turned, 0.0).astype(BF16)


def cross_kernel(factor, home_ref, away_ref, *refs):
    out_ref = refs[-1]
    groups = home_ref.shape[0]
    for g in range(groups):
        values = away_ref[16 * g : 16 * g + 16, :].astype(F32)
        real, imag = spread(values[0:SUB]), spread(values[SUB:])
        left, right = [], []
        for q in range(len(real)):
            left += real[q] + imag[q]
            right += [-t for t in imag[q]] + real[q]
        block = jnp.concatenate([jnp.concatenate(left, 0), jnp.concatenate(right, 0)], 1).astype(BF16)
        product = jnp.dot(home_ref[g], block, preferred_element_type=F32) * factor
        for t in range(SB // 2):
            at = slice(t * LANES, (t + 1) * LANES)
            for c in range(2):
                out_ref[0, 0, c, SUB * g : SUB * g + SUB, at] = product[
                    SUB * t : SUB * t + SUB, c * LANES : (c + 1) * LANES
                ]


def shifted(value, axis, steps):
    size = lax.axis_size(axis)
    return lax.ppermute(value, axis, [(i, (i + steps) % size) for i in range(size)])


def cost(flops, moved):
    return pl.CostEstimate(flops=int(flops), bytes_accessed=int(moved), transcendentals=0)


def whole(*shape):
    return pl.BlockSpec(shape, lambda *_: (0,) * len(shape))


def per_device(raw_counts, seg_valid):
    n_win, n_bin = lax.axis_size("win"), lax.axis_size("bin")
    segs = n_win * n_bin
    samples = raw_counts[:, 0, :]
    rows = samples.shape[0]
    assert rows == LSEG and segs % 2 == 0 and NF % (SUB * segs) == 0
    valid = jnp.concatenate([seg_valid, seg_valid], 1).astype(F32)
    high, low = (jnp.asarray(t) for t in tap_matrix())
    packed = pl.pallas_call(
        decimate_kernel,
        out_shape=jax.ShapeDtypeStruct((PACKED, LANES), BF16),
        scratch_shapes=[pltpu.VMEM((632, high.shape[1]), F32), pltpu.VMEM((616, LANES), F32)],
        cost_estimate=cost(4 * rows * high.size, 2 * (samples.size + 2 * high.size)),
        name="decimate",
    )(samples, valid, high, low)

    mine = [packed] + [shifted(packed, "win", d) for d in range(1, n_win)]
    parts = []
    for value in mine:
        parts += [value] + [shifted(value, "bin", e) for e in range(1, n_bin)]

    transforms, smoothers = tables(segs)
    chunk = lax.axis_index(("win", "bin"))
    transform = lax.dynamic_index_in_dim(jnp.asarray(transforms), chunk, 0, keepdims=False)
    smoother = lax.dynamic_index_in_dim(jnp.asarray(smoothers), chunk, 0, keepdims=False)
    bins = NF // segs
    groups = bins // SUB
    width = segs * SB
    home = pl.pallas_call(
        functools.partial(whiten_kernel, (n_win, n_bin)),
        out_shape=jax.ShapeDtypeStruct((2 * bins, width), BF16),
        scratch_shapes=[pltpu.VMEM((2 * HALF, width), BF16)],
        cost_estimate=cost(2 * transform.size * width, 2 * (transform.size + 3 * bins * width)),
        name="whiten",
    )(*parts, transform, smoother)

    aways = [shifted(home, "blk", offset) for offset in range(1, ROUNDS + 1)]
    depth = segs * 4 * SUB
    tall = SB // 2 * SUB
    turned = pl.pallas_call(
        home_kernel,
        out_shape=jax.ShapeDtypeStruct((groups, tall, depth), BF16),
        cost_estimate=cost(2 * groups * tall * depth * LANES, 2 * groups * tall * depth),
        name="home",
    )(home)

    step = 2 if groups % 2 == 0 else 1
    stacks = None
    for offset in range(ROUNDS):
        extra = [] if stacks is None else [stacks]
        stacks = pl.pallas_call(
            functools.partial(cross_kernel, 1.0 / segs),
            out_shape=jax.ShapeDtypeStruct((ROUNDS, 1, 2, bins, SB * SB), F32),
            grid=(groups // step,),
            in_specs=[
                pl.BlockSpec((step, tall, depth), lambda g: (g, 0, 0)),
                pl.BlockSpec((16 * step, width), lambda g: (g, 0)),
            ]
            + [pl.BlockSpec(memory_space=pl.ANY)] * len(extra),
            out_specs=pl.BlockSpec(
                (1, 1, 2, SUB * step, SB * SB), functools.partial(lambda r, g: (r, 0, 0, g, 0), offset)
            ),
            input_output_aliases={2: 0} if extra else {},
            cost_estimate=cost(4 * groups * tall * depth * LANES, 8 * bins * SB * SB),
            name="cross",
        )(turned, aways[offset], *extra)
    return stacks


def solution(mesh):
    in_specs = (P(("win", "bin"), ("parts", "blk"), None), P(("win", "bin"), ("parts", "blk")))
    out_specs = P(None, ("parts", "blk"), None, ("win", "bin"), None)
    return jax.shard_map(
        per_device, mesh=mesh, in_specs=in_specs, out_specs=out_specs, check_vma=False
    )
```

time: 99.6 us -> 34.4 us (0.35)
  local copies, waits for them, and re-layouts: 39.3 us -> 5.73 us
  other arithmetic: 22.3 us -> 1.31 us
  Pallas kernels: 0 us -> 17.4 us
  matrix products: 15.1 us -> 0 us
  blocking collectives: 11.5 us -> 0 us
  waiting for transfers between devices: 4.08 us -> 1.84 us
  starting transfers between devices: 6.57 us -> 7.65 us
    pallas_call x0 -> x5, Pallas kernels: none -> 17.4 us  [the longest x2 9.37 us: per_device(): pl.pallas_call(functools.partial(cross_kernel, 1.0 / segs), out_shape=jax...]
    dot_general x2 -> x0, local copies, waits for them, and re-layouts: 15.9 us -> none  [cross_block(): jnp.einsum('sfa,sfb->fab', home_spec, away_spec, preferred_element_type=j...]
    dot_general x4 -> x0, matrix products: 15.1 us -> none  [the longest x2 7.41 us: cross_block(): jnp.einsum('sfa,sfb->fab', home_spec, away_spec, preferred_element_type=j...]
    add x3 -> x0, other arithmetic: 11.9 us -> none  [the longest x2 11.9 us: cross_block(): real_part = quarters[:, 0, :, 0, :] + quarters[:, 1, :, 1, :]]
    all_to_all x1 -> x0, blocking collectives: 11.5 us -> none  [per_device(): lax.all_to_all(spectra, ('win', 'bin'), split_axis=1, concat_axis=0, tile...]
    another operation x4 -> x0, local copies, waits for them, and re-layouts: 7.98 us -> none  [cross_block(): jnp.stack([real_part, imag_part], 0).reshape(2, bin_count, SB * SB)]
    slice x3 -> x0, local copies, waits for them, and re-layouts: 7.72 us -> none  [the longest x1 7.31 us: decimate(): window_rows = extended[HIST - offset_back:HIST - offset_back + row_count]]
    reduce_sum x6 -> x0, other arithmetic: 3.96 us -> none  [the longest x4 3.4 us: decimate(): jnp.sum(window_rows * weights[offset_back][None, :, None], axis=1)]
  transfers between devices with their start and end apart: 3 -> 5, of which waited for: 2 -> 2; matrix products, arithmetic and copies ran while one was open for 22% -> 10% of each run, Pallas kernels for 0% -> 20%
where the time goes in v1:
time: 34.4 us; the launch traced here: 33.9 us
  Pallas kernels  17.4 us (51%)
  starting transfers between devices  7.65 us (22%)
  local copies, waits for them, and re-layouts  5.73 us (17%)
  waiting for transfers between devices  1.84 us (5%)
  other arithmetic  1.31 us (4%)
    pallas_call x2, Pallas kernels, per_device(): pl.pallas_call(functools.partial(cross_kernel, 1.0 / segs), out_shape=jax...  9.37 us
    ppermute x5, starting transfers between devices, shifted(): lax.ppermute(value, axis, [(i, (i + steps) % size) for i in range(size)])  7.65 us
    pallas_call x1, Pallas kernels, per_device(): pl.pallas_call(decimate_kernel, out_shape=jax.ShapeDtypeStruct((PACKED, L...  3.4 us
    unnamed x10, local copies, waits for them, and re-layouts  2.49 us
    pallas_call x1, Pallas kernels, per_device(): pl.pallas_call(functools.partial(whiten_kernel, (n_win, n_bin)), out_shap...  2.44 us
    pallas_call x1, Pallas kernels, per_device(): pl.pallas_call(home_kernel, out_shape=jax.ShapeDtypeStruct((groups, tall,...  2.16 us
    ppermute x5, waiting for transfers between devices, shifted(): lax.ppermute(value, axis, [(i, (i + steps) % size) for i in range(size)])  1.84 us
    squeeze x1, local copies, waits for them, and re-layouts, per_device(): lax.dynamic_index_in_dim(jnp.asarray(transforms), chunk, 0, keepdims=False)  1.69 us
  transfers between devices with their start and end apart: 5, of which 2 were waited for; matrix products, arithmetic and copies ran while one was open for 10% of the time, Pallas kernels for 20%

profile of v1, /device:TPU:0, one launch (start us, length us, event | category | flops | bytes accessed | tf_op | source)
XLA Modules:
  0.0 33.9 jit_solution(8352855234078468806)
XLA Ops:
  0.0 1.3 %add_convert_fusion.valid_ref = f32[1,128]{1,0:T(1,128)} fusion(s32[1,64]{1,0:T(1,128)} %param.7), kind=kLoop, calls=%fused_computation.2 | loop fusion | flops 256 | bytes 768 | tf_op jit(solution)/shard_map/convert_element_type | solution.py:230
  1.3 3.4 %decimate.1.refs_0_ = bf16[320,128]{1,0:T(8,128)(2,1)} custom-call(bf16[600,640]{1,0:T(8,128)(2,1)} %bitcast.5, f32[1,128]{1,0:T(1,128)} %add_convert_fusion.valid_ref, bf16[640,512]{1,0:T(8,128)(2,1)} %constant.26.clone.high_ref, bf16[640,512]{1,0:T(8,128)(2,1)} %constant.27.clone.low_ref), custom_call_target="tpu_custom_call" | custom-call | flops 786432000 | bytes 2078720 | tf_op jit(solution)/shard_map/decimate/pallas_call | solution.py:232
  4.7 3.0 %collective-permute-start.1 = (bf16[320,128]{1,0:T(8,128)(2,1)}, bf16[320,128]{1,0:T(8,128)(2,1)S(1)}, u32[]{:S(2)}, u32[]{:S(2)}) collective-permute-start(bf16[320,128]{1,0:T(8,128)(2,1)} %decimate.1.refs_0_), channel_id=1, source_target_pairs={{0,2},{2,0},{1,3},{3,1},{4,6},{6,4},{5,7},{7,5},{8,10},{10,8},{9,1... | collective-permute-start | bytes 245768 | tf_op jit(solution)/shard_map/ppermute | solution.py:213
  7.7 0.0 collective-permute-start
  7.7 1.7 %dynamic-slice_bitcast_fusion.refs_4_ = bf16[224,608]{1,0:T(8,128)(2,1)} fusion(bf16[4,224,608]{2,1,0:T(8,128)(2,1)} %constant.28.clone, s32[]{:T(128)S(6)} %select_n.6), kind=kLoop, calls=%fused_computation | loop fusion | bytes 544772 | tf_op jit(solution)/shard_map/jit(dynamic_index_in_dim)/squeeze | solution.py:247
  9.4 1.0 %collective-permute-done.1.refs_2_ = bf16[320,128]{1,0:T(8,128)(2,1)S(1)} collective-permute-done((bf16[320,128]{1,0:T(8,128)(2,1)}, bf16[320,128]{1,0:T(8,128)(2,1)S(1)}, u32[]{:S(2)}, u32[]{:S(2)}) %collective-permute-start.1) | collective-permute-done | bytes 81952 | tf_op jit(solution)/shard_map/ppermute | solution.py:213
  10.3 0.0 copy-start.1
  10.3 0.0 collective-permute-start.2
  10.3 1.6 %dynamic-slice_bitcast_fusion.1.refs_5_ = bf16[160,224]{1,0:T(8,128)(2,1)} fusion(bf16[4,160,224]{2,1,0:T(8,128)(2,1)} %constant.29.clone, s32[]{:T(128)S(6)} %select_n.6), kind=kLoop, calls=%fused_computation.1 | loop fusion | bytes 143364 | tf_op jit(solution)/shard_map/jit(dynamic_index_in_dim)/squeeze | solution.py:248
  11.9 0.0 collective-permute-done.refs_1_
  11.9 0.0 copy-start.2
  11.9 0.0 collective-permute-done.2.refs_3_
  11.9 0.0 copy-done.1
  11.9 0.6 %copy-done.2 = bf16[320,128]{1,0:T(8,128)(2,1)} copy-done((bf16[320,128]{1,0:T(8,128)(2,1)}, bf16[320,128]{1,0:T(8,128)(2,1)S(1)}, u32[]{:S(2)}) %copy-start.2) | copy-done | bytes 81944
  12.5 0.0 copy-start.3
  12.5 0.6 %copy-done.3 = bf16[320,128]{1,0:T(8,128)(2,1)} copy-done((bf16[320,128]{1,0:T(8,128)(2,1)}, bf16[320,128]{1,0:T(8,128)(2,1)S(1)}, u32[]{:S(2)}) %copy-start.3) | copy-done | bytes 81944
  13.1 2.4 %whiten.1.home_ref = bf16[160,256]{1,0:T(8,128)(2,1)} custom-call(bf16[320,128]{1,0:T(8,128)(2,1)} %decimate.1.refs_0_, bf16[320,128]{1,0:T(8,128)(2,1)} %copy-done.2, bf16[320,128]{1,0:T(8,128)(2,1)} %copy-done.1, bf16[320,128]{1,0:T(8,128)(2,1)} %copy-done.3, bf16[224,608]{1,0:T(8,128)(2,1)} %dynamic-slice_bitcast_fusion.refs_4_, ...), custom_call_target="tpu_custom_call" | custom-call | flops 69730304 | bytes 395264 | tf_op jit(solution)/shard_map/whiten/pallas_call | solution.py:252
  15.6 2.1 %collective-permute-start.4 = (bf16[160,256]{1,0:T(8,128)(2,1)}, bf16[160,256]{1,0:T(8,128)(2,1)S(1)}, u32[]{:S(2)}, u32[]{:S(2)}) collective-permute-start(bf16[160,256]{1,0:T(8,128)(2,1)} %whiten.1.home_ref), channel_id=1, source_target_pairs={{0,4},{4,8},{8,12},{12,0},{1,5},{5,9},{9,13},{13,1},{2,6},{6,10},{... | collective-permute-start | bytes 245768 | tf_op jit(solution)/shard_map/ppermute | solution.py:213
  17.7 2.6 %collective-permute-start.3 = (bf16[160,256]{1,0:T(8,128)(2,1)}, bf16[160,256]{1,0:T(8,128)(2,1)S(1)}, u32[]{:S(2)}, u32[]{:S(2)}) collective-permute-start(bf16[160,256]{1,0:T(8,128)(2,1)} %whiten.1.home_ref), channel_id=1, source_target_pairs={{0,8},{4,12},{8,0},{12,4},{1,9},{5,13},{9,1},{13,5},{2,10},{6,14},... | collective-permute-start | bytes 245768 | tf_op jit(solution)/shard_map/ppermute | solution.py:213
  20.3 2.2 %home.1.home_ref = bf16[10,256,128]{2,1,0:T(8,128)(2,1)} custom-call(bf16[160,256]{1,0:T(8,128)(2,1)} %whiten.1.home_ref), custom_call_target="tpu_custom_call" | custom-call | flops 83886080 | bytes 655360 | tf_op jit(solution)/shard_map/home/pallas_call | solution.py:263
  22.4 0.9 %collective-permute-done.4.away_ref = bf16[160,256]{1,0:T(8,128)(2,1)S(1)} collective-permute-done((bf16[160,256]{1,0:T(8,128)(2,1)}, bf16[160,256]{1,0:T(8,128)(2,1)S(1)}, u32[]{:S(2)}, u32[]{:S(2)}) %collective-permute-start.4) | collective-permute-done | bytes 81952 | tf_op jit(solution)/shard_map/ppermute | solution.py:213
  23.3 0.0 copy-start.4
  23.3 0.6 %copy-done.4 = bf16[160,256]{1,0:T(8,128)(2,1)} copy-done((bf16[160,256]{1,0:T(8,128)(2,1)}, bf16[160,256]{1,0:T(8,128)(2,1)S(1)}, u32[]{:S(2)}) %copy-start.4) | copy-done | bytes 81944
  23.9 4.7 %cross.2.refs_0_ = f32[2,1,2,80,4096]{4,3,2,1,0:T(8,128)} custom-call(bf16[10,256,128]{2,1,0:T(8,128)(2,1)} %home.1.home_ref, bf16[160,256]{1,0:T(8,128)(2,1)} %copy-done.4), custom_call_target="tpu_custom_call" | custom-call | flops 167772160 | bytes 2621440 | tf_op jit(solution)/shard_map/cross/pallas_call | solution.py:274
  28.6 0.0 collective-permute-done.3.away_ref
  28.6 0.0 copy-start
  28.6 0.6 %copy-done = bf16[160,256]{1,0:T(8,128)(2,1)} copy-done((bf16[160,256]{1,0:T(8,128)(2,1)}, bf16[160,256]{1,0:T(8,128)(2,1)S(1)}, u32[]{:S(2)}) %copy-start) | copy-done | bytes 81944
  29.2 4.7 %cross.3 = f32[2,1,2,80,4096]{4,3,2,1,0:T(8,128)} custom-call(bf16[10,256,128]{2,1,0:T(8,128)(2,1)} %home.1.home_ref, bf16[160,256]{1,0:T(8,128)(2,1)} %copy-done, f32[2,1,2,80,4096]{4,3,2,1,0:T(8,128)} %cross.2.refs_0_), custom_call_target="tpu_custom_call", output_to_operand_aliasing={{}: (2, {})} | custom-call | flops 167772160 | bytes 2621440 | tf_op jit(solution)/shard_map/cross/pallas_call | solution.py:274
Async XLA Ops:
  4.7 5.6 %collective-permute-start.1 = (bf16[320,128]{1,0:T(8,128)(2,1)}, bf16[320,128]{1,0:T(8,128)(2,1)S(1)}, u32[]{:S(2)}, u32[]{:S(2)}) collective-permute-start(bf16[320,128]{1,0:T(8,128)(2,1)} %decimate.1.refs_0_), channel_id=1, source_target_pairs={{0,2},{2,0},{1,3},{3,1},{4,6},{6,4},{5,7},{7,5},{8,10},{10,8},{9,1... | collective-permute-start | bytes 245768 | tf_op jit(solution)/shard_map/ppermute | solution.py:213
  7.7 4.2 %collective-permute-start = (bf16[320,128]{1,0:T(8,128)(2,1)}, bf16[320,128]{1,0:T(8,128)(2,1)S(1)}, u32[]{:S(2)}, u32[]{:S(2)}) collective-permute-start(bf16[320,128]{1,0:T(8,128)(2,1)} %decimate.1.refs_0_), channel_id=1, source_target_pairs={{0,1},{1,0},{2,3},{3,2},{4,5},{5,4},{6,7},{7,6},{8,9},{9,8},{10,11... | collective-permute-start | bytes 245768 | tf_op jit(solution)/shard_map/ppermute | solution.py:213
  10.3 1.6 %copy-start.1 = (bf16[320,128]{1,0:T(8,128)(2,1)}, bf16[320,128]{1,0:T(8,128)(2,1)S(1)}, u32[]{:S(2)}) copy-start(bf16[320,128]{1,0:T(8,128)(2,1)S(1)} %collective-permute-done.1.refs_2_) | copy-start | bytes 245764
  10.3 1.6 %collective-permute-start.2 = (bf16[320,128]{1,0:T(8,128)(2,1)S(1)}, bf16[320,128]{1,0:T(8,128)(2,1)S(1)}, u32[]{:S(2)}, u32[]{:S(2)}) collective-permute-start(bf16[320,128]{1,0:T(8,128)(2,1)S(1)} %collective-permute-done.1.refs_2_), channel_id=1, source_target_pairs={{0,1},{1,0},{2,3},{3,2},{4,5},{5,4},{6,7},{7,6},{8,9},{9,8},{10,11... | collective-permute-start | bytes 245768 | tf_op jit(solution)/shard_map/ppermute | solution.py:213
  11.9 0.6 %copy-start.2 = (bf16[320,128]{1,0:T(8,128)(2,1)}, bf16[320,128]{1,0:T(8,128)(2,1)S(1)}, u32[]{:S(2)}) copy-start(bf16[320,128]{1,0:T(8,128)(2,1)S(1)} %collective-permute-done.refs_1_) | copy-start | bytes 245764
  12.5 0.6 %copy-start.3 = (bf16[320,128]{1,0:T(8,128)(2,1)}, bf16[320,128]{1,0:T(8,128)(2,1)S(1)}, u32[]{:S(2)}) copy-start(bf16[320,128]{1,0:T(8,128)(2,1)S(1)} %collective-permute-done.2.refs_3_) | copy-start | bytes 245764
  15.6 7.7 %collective-permute-start.4 = (bf16[160,256]{1,0:T(8,128)(2,1)}, bf16[160,256]{1,0:T(8,128)(2,1)S(1)}, u32[]{:S(2)}, u32[]{:S(2)}) collective-permute-start(bf16[160,256]{1,0:T(8,128)(2,1)} %whiten.1.home_ref), channel_id=1, source_target_pairs={{0,4},{4,8},{8,12},{12,0},{1,5},{5,9},{9,13},{13,1},{2,6},{6,10},{... | collective-permute-start | bytes 245768 | tf_op jit(solution)/shard_map/ppermute | solution.py:213
  17.7 10.9 %collective-permute-start.3 = (bf16[160,256]{1,0:T(8,128)(2,1)}, bf16[160,256]{1,0:T(8,128)(2,1)S(1)}, u32[]{:S(2)}, u32[]{:S(2)}) collective-permute-start(bf16[160,256]{1,0:T(8,128)(2,1)} %whiten.1.home_ref), channel_id=1, source_target_pairs={{0,8},{4,12},{8,0},{12,4},{1,9},{5,13},{9,1},{13,5},{2,10},{6,14},... | collective-permute-start | bytes 245768 | tf_op jit(solution)/shard_map/ppermute | solution.py:213
  23.3 0.6 %copy-start.4 = (bf16[160,256]{1,0:T(8,128)(2,1)}, bf16[160,256]{1,0:T(8,128)(2,1)S(1)}, u32[]{:S(2)}) copy-start(bf16[160,256]{1,0:T(8,128)(2,1)S(1)} %collective-permute-done.4.away_ref) | copy-start | bytes 245764
  28.6 0.6 %copy-start = (bf16[160,256]{1,0:T(8,128)(2,1)}, bf16[160,256]{1,0:T(8,128)(2,1)S(1)}, u32[]{:S(2)}) copy-start(bf16[160,256]{1,0:T(8,128)(2,1)S(1)} %collective-permute-done.3.away_ref) | copy-start | bytes 245764

commit v2 on v1

--- a/solution.py
+++ b/solution.py
@@ -36,17 +36,16 @@
     return 2.0 * cutoff * shaped * window
 
 
-def tap_matrix():
+def taps():
     coeffs = filter_coeffs()
-    weights = np.zeros((DECIM, HIST + 1))
+    weights = np.zeros((DECIM, HIST + 1), np.float32)
     for p in range(DECIM):
         for o in range(HIST + 1):
             t = DECIM * o - p
             if 0 <= t < TAPS:
                 weights[p, o] = coeffs[t]
-    full = np.kron(weights, np.eye(SB)).astype(np.float32)
-    high = full.astype(BF16)
-    low = (full - high.astype(np.float32)).astype(BF16)
+    high = weights.astype(BF16).astype(np.float32)
+    low = (weights - high).astype(BF16).astype(np.float32)
     return high, low
 
 
@@ -84,13 +83,34 @@
     return pltpu.roll(value, SB, 1)
 
 
-def decimate_kernel(x_ref, valid_ref, high_ref, low_ref, out_ref, y_ref, e_ref):
+def decimate_kernel(
+    x_hbm, valid_hbm, table_hbm, smooth_hbm, out_ref, table_ref, smooth_ref, x_ref, valid_ref, tap_ref, y_ref, e_ref, sem
+):
     rows = x_ref.shape[0]
-    x = x_ref[...]
+    chunk = lax.axis_index("win") * lax.axis_size("bin") + lax.axis_index("bin")
+    copies = [
+        pltpu.make_async_copy(x_hbm, x_ref, sem.at[0]),
+        pltpu.make_async_copy(valid_hbm, valid_ref, sem.at[1]),
+        pltpu.make_async_copy(table_hbm.at[chunk], table_ref, sem.at[2]),
+        pltpu.make_async_copy(smooth_hbm.at[chunk], smooth_ref, sem.at[3]),
+    ]
+    for copy in copies:
+        copy.start()
+    row = lax.broadcasted_iota(jnp.int32, (SB, LANES), 0)
+    lane = lax.broadcasted_iota(jnp.int32, (SB, LANES), 1)
+    same, low = lane % SB == row, lane < SB
+    zero = jnp.zeros((SB, LANES), F32)
+    for part, values in enumerate(taps()):
+        for p in range(DECIM):
+            for j in range((HIST + 1) // 2):
+                pair = jnp.where(low, float(values[p, 2 * j]), float(values[p, 2 * j + 1]))
+                tap_ref[part, p * SB : (p + 1) * SB, j * LANES : (j + 1) * LANES] = jnp.where(same, pair, zero).astype(BF16)
     y_ref[0:16, :] = jnp.zeros((16, y_ref.shape[1]), F32)
     y_ref[16 + rows :, :] = jnp.zeros((y_ref.shape[0] - 16 - rows, y_ref.shape[1]), F32)
-    y_ref[16 : 16 + rows, :] = jnp.dot(x, high_ref[...], preferred_element_type=F32) + jnp.dot(
-        x, low_ref[...], preferred_element_type=F32
+    copies[0].wait()
+    x = x_ref[...]
+    y_ref[16 : 16 + rows, :] = jnp.dot(x, tap_ref[0], preferred_element_type=F32) + jnp.dot(
+        x, tap_ref[1], preferred_element_type=F32
     )
     total = y_ref[8 : 8 + 616, 0:LANES]
     for j in range(1, (HIST + 1) // 2):
@@ -103,8 +123,12 @@
     out_ref[0:HALF, :] = rounded
     rest = value - rounded.astype(F32)
     ends = jnp.where(low_lanes((SUB, LANES)), rest[0:SUB], rest[HALF - SUB : HALF])
-    valid = jnp.broadcast_to(valid_ref[...], (SUB, LANES))
+    copies[1].wait()
+    valid = valid_ref[...].astype(F32)
+    valid = jnp.broadcast_to(jnp.concatenate([valid, valid], 1), (SUB, LANES))
     out_ref[HALF:PACKED, :] = jnp.concatenate([ends, valid], 0).astype(BF16)
+    copies[2].wait()
+    copies[3].wait()
 
 
 def whiten_kernel(sizes, *refs):
@@ -188,9 +212,10 @@
         out_ref[g] = jnp.where(diagonal, turned, 0.0).astype(BF16)
 
 
-def cross_kernel(factor, home_ref, away_ref, *refs):
-    out_ref = refs[-1]
+def cross_kernel(offset, factor, home_ref, away_ref, *refs):
+    out_hbm, out_ref, sem = refs[-3:]
     groups = home_ref.shape[0]
+    copies = []
     for g in range(groups):
         values = away_ref[16 * g : 16 * g + 16, :].astype(F32)
         real, imag = spread(values[0:SUB]), spread(values[SUB:])
@@ -200,12 +225,16 @@
             right += [-t for t in imag[q]] + real[q]
         block = jnp.concatenate([jnp.concatenate(left, 0), jnp.concatenate(right, 0)], 1).astype(BF16)
         product = jnp.dot(home_ref[g], block, preferred_element_type=F32) * factor
-        for t in range(SB // 2):
-            at = slice(t * LANES, (t + 1) * LANES)
-            for c in range(2):
-                out_ref[0, 0, c, SUB * g : SUB * g + SUB, at] = product[
+        at = pl.ds(SUB * g, SUB)
+        for c in range(2):
+            for t in range(SB // 2):
+                out_ref[c, SUB * g : SUB * g + SUB, t * LANES : (t + 1) * LANES] = product[
                     SUB * t : SUB * t + SUB, c * LANES : (c + 1) * LANES
                 ]
+            copies.append(pltpu.make_async_copy(out_ref.at[c, at], out_hbm.at[offset, 0, c, at], sem.at[2 * g + c]))
+            copies[-1].start()
+    for copy in copies:
+        copy.wait()
 
 
 def shifted(value, axis, steps):
@@ -217,8 +246,12 @@
     return pl.CostEstimate(flops=int(flops), bytes_accessed=int(moved), transcendentals=0)
 
 
-def whole(*shape):
-    return pl.BlockSpec(shape, lambda *_: (0,) * len(shape))
+def room(limit):
+    return pltpu.CompilerParams(vmem_limit_bytes=limit)
+
+
+VMEM = pl.BlockSpec(memory_space=pltpu.VMEM)
+HBM = pl.BlockSpec(memory_space=pl.ANY)
 
 
 def per_device(raw_counts, seg_valid):
@@ -227,33 +260,46 @@
     samples = raw_counts[:, 0, :]
     rows = samples.shape[0]
     assert rows == LSEG and segs % 2 == 0 and NF % (SUB * segs) == 0
-    valid = jnp.concatenate([seg_valid, seg_valid], 1).astype(F32)
-    high, low = (jnp.asarray(t) for t in tap_matrix())
-    packed = pl.pallas_call(
+    transforms, smoothers = tables(segs)
+    wide = (HIST + 1) * SB
+    packed, transform, smoother = pl.pallas_call(
         decimate_kernel,
-        out_shape=jax.ShapeDtypeStruct((PACKED, LANES), BF16),
-        scratch_shapes=[pltpu.VMEM((632, high.shape[1]), F32), pltpu.VMEM((616, LANES), F32)],
-        cost_estimate=cost(4 * rows * high.size, 2 * (samples.size + 2 * high.size)),
+        out_shape=(
+            jax.ShapeDtypeStruct((PACKED, LANES), BF16),
+            jax.ShapeDtypeStruct(transforms.shape[1:], BF16),
+            jax.ShapeDtypeStruct(smoothers.shape[1:], BF16),
+        ),
+        in_specs=[pl.BlockSpec(memory_space=pltpu.HBM)] * 4,
+        out_specs=(VMEM,) * 3,
+        scratch_shapes=[
+            pltpu.VMEM(samples.shape, BF16),
+            pltpu.VMEM(seg_valid.shape, jnp.int32),
+            pltpu.VMEM((2, DECIM * SB, wide), BF16),
+            pltpu.VMEM((632, wide), F32),
+            pltpu.VMEM((616, LANES), F32),
+            pltpu.SemaphoreType.DMA((4,)),
+        ],
+        cost_estimate=cost(4 * rows * DECIM * SB * wide, 2 * samples.size),
+        compiler_params=room(16 << 20),
         name="decimate",
-    )(samples, valid, high, low)
+    )(*(pltpu.with_memory_space_constraint(v, pltpu.HBM) for v in (samples, seg_valid, jnp.asarray(transforms), jnp.asarray(smoothers))))
 
     mine = [packed] + [shifted(packed, "win", d) for d in range(1, n_win)]
     parts = []
     for value in mine:
         parts += [value] + [shifted(value, "bin", e) for e in range(1, n_bin)]
 
-    transforms, smoothers = tables(segs)
-    chunk = lax.axis_index(("win", "bin"))
-    transform = lax.dynamic_index_in_dim(jnp.asarray(transforms), chunk, 0, keepdims=False)
-    smoother = lax.dynamic_index_in_dim(jnp.asarray(smoothers), chunk, 0, keepdims=False)
     bins = NF // segs
     groups = bins // SUB
     width = segs * SB
     home = pl.pallas_call(
         functools.partial(whiten_kernel, (n_win, n_bin)),
         out_shape=jax.ShapeDtypeStruct((2 * bins, width), BF16),
+        in_specs=[VMEM] * (segs + 2),
+        out_specs=VMEM,
         scratch_shapes=[pltpu.VMEM((2 * HALF, width), BF16)],
         cost_estimate=cost(2 * transform.size * width, 2 * (transform.size + 3 * bins * width)),
+        compiler_params=room(6 << 20),
         name="whiten",
     )(*parts, transform, smoother)
 
@@ -263,28 +309,25 @@
     turned = pl.pallas_call(
         home_kernel,
         out_shape=jax.ShapeDtypeStruct((groups, tall, depth), BF16),
+        in_specs=[VMEM],
+        out_specs=VMEM,
         cost_estimate=cost(2 * groups * tall * depth * LANES, 2 * groups * tall * depth),
+        compiler_params=room(6 << 20),
         name="home",
     )(home)
 
-    step = 2 if groups % 2 == 0 else 1
     stacks = None
     for offset in range(ROUNDS):
         extra = [] if stacks is None else [stacks]
         stacks = pl.pallas_call(
-            functools.partial(cross_kernel, 1.0 / segs),
+            functools.partial(cross_kernel, offset, 1.0 / segs),
             out_shape=jax.ShapeDtypeStruct((ROUNDS, 1, 2, bins, SB * SB), F32),
-            grid=(groups // step,),
-            in_specs=[
-                pl.BlockSpec((step, tall, depth), lambda g: (g, 0, 0)),
-                pl.BlockSpec((16 * step, width), lambda g: (g, 0)),
-            ]
-            + [pl.BlockSpec(memory_space=pl.ANY)] * len(extra),
-            out_specs=pl.BlockSpec(
-                (1, 1, 2, SUB * step, SB * SB), functools.partial(lambda r, g: (r, 0, 0, g, 0), offset)
-            ),
+            in_specs=[VMEM] * 2 + [HBM] * len(extra),
+            out_specs=HBM,
+            scratch_shapes=[pltpu.VMEM((2, bins, SB * SB), F32), pltpu.SemaphoreType.DMA((2 * groups,))],
             input_output_aliases={2: 0} if extra else {},
             cost_estimate=cost(4 * groups * tall * depth * LANES, 8 * bins * SB * SB),
+            compiler_params=room(8 << 20),
             name="cross",
         )(turned, aways[offset], *extra)
     return stacks

time: 34.4 us -> 22.4 us (0.65); the launches traced: 33.9 us -> 22.3 us
  Pallas kernels: 17.4 us -> 7.42 us
  local copies, waits for them, and re-layouts: 5.73 us -> 0 us
  waiting for transfers between devices: 1.84 us -> 7.07 us
  other arithmetic: 1.31 us -> 0 us
    pallas_call x3, Pallas kernels: 12.8 us -> 6.35 us  [the longest x2 3.87 us: per_device(): pl.pallas_call(functools.partial(cross_kernel, offset, 1.0 / segs), out_s...]
    ppermute x5, waiting for transfers between devices: 1.84 us -> 7.07 us  [shifted(): lax.ppermute(value, axis, [(i, (i + steps) % size) for i in range(size)])]
    squeeze x2 -> x0, local copies, waits for them, and re-layouts: 3.24 us -> none  [the longest x1 1.69 us: per_device(): lax.dynamic_index_in_dim(jnp.asarray(transforms), chunk, 0, keepdims=False)]
    unnamed x10 -> x0, local copies, waits for them, and re-layouts: 2.49 us -> none
    pallas_call x1, Pallas kernels: 2.44 us -> 0.67 us  [per_device(): pl.pallas_call(functools.partial(whiten_kernel, (n_win, n_bin)), out_shap...]
    pallas_call x1, Pallas kernels: 2.16 us -> 0.4 us  [per_device(): pl.pallas_call(home_kernel, out_shape=jax.ShapeDtypeStruct((groups, tall,...]
    convert_element_type x1 -> x0, other arithmetic: 1.31 us -> none  [per_device(): valid = jnp.concatenate([seg_valid, seg_valid], 1).astype(F32)]
  transfers between devices with their start and end apart: 5 -> 5, of which waited for: 2 -> 4; matrix products, arithmetic and copies ran while one was open for 10% -> 0% of each run, Pallas kernels for 20% -> 10%
where the time goes in v2:
time: 22.4 us; the launch traced here: 22.3 us
  starting transfers between devices  7.76 us (35%)
  Pallas kernels  7.42 us (33%)
  waiting for transfers between devices  7.07 us (32%)
    ppermute x5, starting transfers between devices, shifted(): lax.ppermute(value, axis, [(i, (i + steps) % size) for i in range(size)])  7.76 us
    ppermute x5, waiting for transfers between devices, shifted(): lax.ppermute(value, axis, [(i, (i + steps) % size) for i in range(size)])  7.07 us
    pallas_call x2, Pallas kernels, per_device(): pl.pallas_call(functools.partial(cross_kernel, offset, 1.0 / segs), out_s...  3.87 us
    pallas_call x1, Pallas kernels, per_device(): pl.pallas_call(decimate_kernel, out_shape=(jax.ShapeDtypeStruct((PACKED,...  2.48 us
    pallas_call x1, Pallas kernels, per_device(): pl.pallas_call(functools.partial(whiten_kernel, (n_win, n_bin)), out_shap...  0.67 us
  transfers between devices with their start and end apart: 5, of which 4 were waited for; matrix products, arithmetic and copies ran while one was open for 0% of the time, Pallas kernels for 10%

profile of v2, /device:TPU:0, one launch (start us, length us, event | category | flops | bytes accessed | tf_op | source)
XLA Modules:
  0.0 22.3 jit_solution(15752118500014450380)
XLA Ops:
  0.0 2.5 %decimate.1 = (bf16[320,128]{1,0:T(8,128)(2,1)S(1)}, bf16[224,608]{1,0:T(8,128)(2,1)S(1)}, bf16[160,224]{1,0:T(8,128)(2,1)S(1)}) custom-call(bf16[600,640]{1,0:T(8,128)(2,1)} %bitcast.1, s32[1,64]{1,0:T(1,128)} %valid_hbm.1, bf16[4,224,608]{2,1,0:T(8,128)(2,1)} %constant.4.clone.table_hbm, bf16[4,160,224]{2,1,0:T(8,128)(2,1)} %constant.5.clone.smooth_hbm), custom_call_target="tpu_custom_call" | custom-call | flops 786432000 | bytes 768000 | tf_op jit(solution)/shard_map/decimate/pallas_call | solution.py:265
  2.5 3.0 %collective-permute-start.1 = (bf16[320,128]{1,0:T(8,128)(2,1)S(1)}, bf16[320,128]{1,0:T(8,128)(2,1)S(1)}, u32[]{:S(2)}, u32[]{:S(2)}) collective-permute-start(bf16[320,128]{1,0:T(8,128)(2,1)S(1)} %get-tuple-element.8.refs_0_), channel_id=1, source_target_pairs={{0,2},{2,0},{1,3},{3,1},{4,6},{6,4},{5,7},{7,5},{8,10},{10,8},{9,1... | collective-permute-start | bytes 245768 | tf_op jit(solution)/shard_map/ppermute | solution.py:242
  5.5 0.0 collective-permute-start
  5.5 2.4 %collective-permute-done.1.refs_2_ = bf16[320,128]{1,0:T(8,128)(2,1)S(1)} collective-permute-done((bf16[320,128]{1,0:T(8,128)(2,1)S(1)}, bf16[320,128]{1,0:T(8,128)(2,1)S(1)}, u32[]{:S(2)}, u32[]{:S(2)}) %collective-permute-start.1) | collective-permute-done | bytes 81952 | tf_op jit(solution)/shard_map/ppermute | solution.py:242
  8.0 0.0 collective-permute-start.2
  8.0 0.0 collective-permute-done.refs_1_
  8.0 1.3 %collective-permute-done.2.refs_3_ = bf16[320,128]{1,0:T(8,128)(2,1)S(1)} collective-permute-done((bf16[320,128]{1,0:T(8,128)(2,1)S(1)}, bf16[320,128]{1,0:T(8,128)(2,1)S(1)}, u32[]{:S(2)}, u32[]{:S(2)}) %collective-permute-start.2) | collective-permute-done | bytes 81952 | tf_op jit(solution)/shard_map/ppermute | solution.py:242
  9.2 0.7 %whiten.1.home_ref = bf16[160,256]{1,0:T(8,128)(2,1)S(1)} custom-call(bf16[320,128]{1,0:T(8,128)(2,1)S(1)} %get-tuple-element.8.refs_0_, bf16[320,128]{1,0:T(8,128)(2,1)S(1)} %collective-permute-done.refs_1_, bf16[320,128]{1,0:T(8,128)(2,1)S(1)} %collective-permute-done.1.refs_2_, bf16[320,128]{1,0:T(8,128)(2,1)S(1)} %collective-permute-done.2.refs_3_, ...), custom_call_target="tpu_custom_call" | custom-call | flops 69730304 | bytes 395264 | tf_op jit(solution)/shard_map/whiten/pallas_call | solution.py:295
  9.9 2.1 %collective-permute-start.4 = (bf16[160,256]{1,0:T(8,128)(2,1)S(1)}, bf16[160,256]{1,0:T(8,128)(2,1)S(1)}, u32[]{:S(2)}, u32[]{:S(2)}) collective-permute-start(bf16[160,256]{1,0:T(8,128)(2,1)S(1)} %whiten.1.home_ref), channel_id=1, source_target_pairs={{0,4},{4,8},{8,12},{12,0},{1,5},{5,9},{9,13},{13,1},{2,6},{6,10},{... | collective-permute-start | bytes 245768 | tf_op jit(solution)/shard_map/ppermute | solution.py:242
  12.1 2.6 %collective-permute-start.3 = (bf16[160,256]{1,0:T(8,128)(2,1)S(1)}, bf16[160,256]{1,0:T(8,128)(2,1)S(1)}, u32[]{:S(2)}, u32[]{:S(2)}) collective-permute-start(bf16[160,256]{1,0:T(8,128)(2,1)S(1)} %whiten.1.home_ref), channel_id=1, source_target_pairs={{0,8},{4,12},{8,0},{12,4},{1,9},{5,13},{9,1},{13,5},{2,10},{6,14},... | collective-permute-start | bytes 245768 | tf_op jit(solution)/shard_map/ppermute | solution.py:242
  14.6 0.4 %home.1.home_ref = bf16[10,256,128]{2,1,0:T(8,128)(2,1)S(1)} custom-call(bf16[160,256]{1,0:T(8,128)(2,1)S(1)} %whiten.1.home_ref), custom_call_target="tpu_custom_call" | custom-call | flops 83886080 | bytes 655360 | tf_op jit(solution)/shard_map/home/pallas_call | solution.py:309
  15.1 2.3 %collective-permute-done.4.away_ref = bf16[160,256]{1,0:T(8,128)(2,1)S(1)} collective-permute-done((bf16[160,256]{1,0:T(8,128)(2,1)S(1)}, bf16[160,256]{1,0:T(8,128)(2,1)S(1)}, u32[]{:S(2)}, u32[]{:S(2)}) %collective-permute-start.4) | collective-permute-done | bytes 81952 | tf_op jit(solution)/shard_map/ppermute | solution.py:242
  17.3 1.9 %cross.2.refs_0_ = f32[2,1,2,80,4096]{4,3,2,1,0:T(8,128)} custom-call(bf16[10,256,128]{2,1,0:T(8,128)(2,1)S(1)} %home.1.home_ref, bf16[160,256]{1,0:T(8,128)(2,1)S(1)} %collective-permute-done.4.away_ref), custom_call_target="tpu_custom_call" | custom-call | flops 167772160 | bytes 2621440 | tf_op jit(solution)/shard_map/cross/pallas_call | solution.py:322
  19.3 1.1 %collective-permute-done.3.away_ref = bf16[160,256]{1,0:T(8,128)(2,1)S(1)} collective-permute-done((bf16[160,256]{1,0:T(8,128)(2,1)S(1)}, bf16[160,256]{1,0:T(8,128)(2,1)S(1)}, u32[]{:S(2)}, u32[]{:S(2)}) %collective-permute-start.3) | collective-permute-done | bytes 81952 | tf_op jit(solution)/shard_map/ppermute | solution.py:242
  20.4 1.9 %cross.3 = f32[2,1,2,80,4096]{4,3,2,1,0:T(8,128)} custom-call(bf16[10,256,128]{2,1,0:T(8,128)(2,1)S(1)} %home.1.home_ref, bf16[160,256]{1,0:T(8,128)(2,1)S(1)} %collective-permute-done.3.away_ref, f32[2,1,2,80,4096]{4,3,2,1,0:T(8,128)} %cross.2.refs_0_), custom_call_target="tpu_custom_call", output_to_operand_aliasing={{}: (2, {})} | custom-call | flops 167772160 | bytes 2621440 | tf_op jit(solution)/shard_map/cross/pallas_call | solution.py:322
Async XLA Ops:
  2.5 5.5 %collective-permute-start.1 = (bf16[320,128]{1,0:T(8,128)(2,1)S(1)}, bf16[320,128]{1,0:T(8,128)(2,1)S(1)}, u32[]{:S(2)}, u32[]{:S(2)}) collective-permute-start(bf16[320,128]{1,0:T(8,128)(2,1)S(1)} %get-tuple-element.8.refs_0_), channel_id=1, source_target_pairs={{0,2},{2,0},{1,3},{3,1},{4,6},{6,4},{5,7},{7,5},{8,10},{10,8},{9,1... | collective-permute-start | bytes 245768 | tf_op jit(solution)/shard_map/ppermute | solution.py:242
  5.5 2.4 %collective-permute-start = (bf16[320,128]{1,0:T(8,128)(2,1)S(1)}, bf16[320,128]{1,0:T(8,128)(2,1)S(1)}, u32[]{:S(2)}, u32[]{:S(2)}) collective-permute-start(bf16[320,128]{1,0:T(8,128)(2,1)S(1)} %get-tuple-element.8.refs_0_), channel_id=1, source_target_pairs={{0,1},{1,0},{2,3},{3,2},{4,5},{5,4},{6,7},{7,6},{8,9},{9,8},{10,11... | collective-permute-start | bytes 245768 | tf_op jit(solution)/shard_map/ppermute | solution.py:242
  8.0 1.3 %collective-permute-start.2 = (bf16[320,128]{1,0:T(8,128)(2,1)S(1)}, bf16[320,128]{1,0:T(8,128)(2,1)S(1)}, u32[]{:S(2)}, u32[]{:S(2)}) collective-permute-start(bf16[320,128]{1,0:T(8,128)(2,1)S(1)} %collective-permute-done.1.refs_2_), channel_id=1, source_target_pairs={{0,1},{1,0},{2,3},{3,2},{4,5},{5,4},{6,7},{7,6},{8,9},{9,8},{10,11... | collective-permute-start | bytes 245768 | tf_op jit(solution)/shard_map/ppermute | solution.py:242
  9.9 7.4 %collective-permute-start.4 = (bf16[160,256]{1,0:T(8,128)(2,1)S(1)}, bf16[160,256]{1,0:T(8,128)(2,1)S(1)}, u32[]{:S(2)}, u32[]{:S(2)}) collective-permute-start(bf16[160,256]{1,0:T(8,128)(2,1)S(1)} %whiten.1.home_ref), channel_id=1, source_target_pairs={{0,4},{4,8},{8,12},{12,0},{1,5},{5,9},{9,13},{13,1},{2,6},{6,10},{... | collective-permute-start | bytes 245768 | tf_op jit(solution)/shard_map/ppermute | solution.py:242
  12.1 8.3 %collective-permute-start.3 = (bf16[160,256]{1,0:T(8,128)(2,1)S(1)}, bf16[160,256]{1,0:T(8,128)(2,1)S(1)}, u32[]{:S(2)}, u32[]{:S(2)}) collective-permute-start(bf16[160,256]{1,0:T(8,128)(2,1)S(1)} %whiten.1.home_ref), channel_id=1, source_target_pairs={{0,8},{4,12},{8,0},{12,4},{1,9},{5,13},{9,1},{13,5},{2,10},{6,14},... | collective-permute-start | bytes 245768 | tf_op jit(solution)/shard_map/ppermute | solution.py:242

commit v3 on v2

v3 whole, which is shorter than its diff:
```python
import functools
import math

import jax
import jax.numpy as jnp
import numpy as np
from jax import lax
from jax.experimental import pallas as pl
from jax.experimental.pallas import tpu as pltpu
from jax.sharding import PartitionSpec as P

SB = 64
LSEG = 600
NF = 320
DECIM = 10
TAPS = 64
SMOOTH = 33
ROUNDS = 2
HIST = 7

EPSILON = 1e-06
LANES = 128
SUB = 8
HALF = 320
CHUNK = 32
BACK = 16
BF16 = jnp.bfloat16
F32 = jnp.float32


def filter_coeffs():
    position = np.arange(TAPS, dtype=np.float64)
    centre = 0.5 * (TAPS - 1)
    cutoff = 0.4 / DECIM
    shaped = np.sinc(2.0 * cutoff * (position - centre))
    window = 0.54 - 0.46 * np.cos(2.0 * math.pi * position / (TAPS - 1))
    return 2.0 * cutoff * shaped * window


def taps():
    coeffs = filter_coeffs()
    weights = np.zeros((DECIM, HIST + 1), np.float32)
    for p in range(DECIM):
        for o in range(HIST + 1):
            t = DECIM * o - p
            if 0 <= t < TAPS:
                weights[p, o] = coeffs[t]
    high = weights.astype(BF16).astype(np.float32)
    low = (weights - high).astype(BF16).astype(np.float32)
    return high, low


def tap_matrix():
    out = np.zeros((2, 2, CHUNK, DECIM // 2, BACK + CHUNK), np.float32)
    for part, values in enumerate(taps()):
        for p in range(DECIM):
            for o in range(HIST + 1):
                for n in range(CHUNK):
                    out[part, p % 2, n, p // 2, BACK + n - o] = values[p, o]
    return out.reshape(4 * CHUNK, DECIM // 2 * (BACK + CHUNK)).astype(BF16)


def window(count):
    return count + SMOOTH - 1


def phases(bins, samples):
    return ((bins[:, None] + 1) * samples[None, :] % (2 * LSEG)) * (math.pi / LSEG)


def transform_table():
    samples = np.arange(2 * HALF)
    radians = phases(np.arange(NF), samples)
    inside = samples[None, :] < LSEG
    parts = [np.where(inside, np.cos(radians), 0.0), np.where(inside, -np.sin(radians), 0.0)]
    return np.concatenate(parts, 1).astype(BF16)


def window_tables(chunks):
    count = NF // chunks
    width = window(count)
    assert width <= LANES
    out = np.zeros((chunks, width + count, LANES), np.float32)
    for chunk in range(chunks):
        start = min(max(chunk * count - SMOOTH // 2, 0), NF - width)
        bins = np.arange(start, start + width)
        radians = phases(bins, np.arange(SUB))
        first = np.concatenate([np.cos(radians), -np.sin(radians)], 1)
        out[chunk, :width, : 4 * SUB] = np.concatenate([first, first], 1)
        own = np.arange(chunk * count, (chunk + 1) * count)
        low = np.clip(own - SMOOTH // 2, 0, NF - SMOOTH)
        out[chunk, width:, :width] = (bins[None, :] >= low[:, None]) & (bins[None, :] < low[:, None] + SMOOTH)
    return out.astype(BF16)


def low_lanes(shape):
    return lax.broadcasted_iota(jnp.int32, shape, len(shape) - 1) % LANES < SB


def swap(value):
    return pltpu.roll(value, SB, 1)


def spread(tile):
    low = low_lanes(tile.shape)
    zero = jnp.zeros(tile.shape, F32)
    other = swap(tile)
    return [
        jnp.where(low, tile, zero),
        jnp.where(low, zero, other),
        jnp.where(low, other, zero),
        jnp.where(low, zero, tile),
    ]


def window_start(chunk, count):
    return jnp.clip(chunk * count - SMOOTH // 2, 0, NF - window(count))


def segment_kernel(sizes, x_hbm, taps_hbm, valid_hbm, table_hbm, windows_hbm, *refs):
    n_win, n_bin = sizes
    segs = n_win * n_bin
    outs, (windows_ref, x_ref, taps_ref, valid_ref, table_ref, s_ref, sem) = refs[:segs], refs[segs:]
    rows = x_hbm.shape[0]
    my_win, my_bin = lax.axis_index("win"), lax.axis_index("bin")
    x_ref[0:BACK, :] = jnp.zeros((BACK, x_ref.shape[1]), BF16)
    x_ref[BACK + rows :, :] = jnp.zeros((x_ref.shape[0] - BACK - rows, x_ref.shape[1]), BF16)
    copies = [
        pltpu.make_async_copy(x_hbm, x_ref.at[pl.ds(BACK, rows)], sem.at[0]),
        pltpu.make_async_copy(taps_hbm, taps_ref, sem.at[1]),
        pltpu.make_async_copy(valid_hbm, valid_ref, sem.at[2]),
        pltpu.make_async_copy(table_hbm, table_ref, sem.at[3]),
        pltpu.make_async_copy(windows_hbm.at[my_win * n_bin + my_bin], windows_ref, sem.at[4]),
    ]
    for copy in copies:
        copy.start()
    copies[1].wait()
    copies[0].wait()
    matrix = taps_ref[...]
    low = low_lanes((CHUNK, LANES))
    chunks = []
    for c in range(HALF // CHUNK):
        sides = []
        for start in (c * CHUNK, c * CHUNK + HALF):
            window_rows = x_ref[start : start + BACK + CHUNK, :]
            sides.append(
                jnp.concatenate([window_rows[:, t * LANES : (t + 1) * LANES] for t in range(DECIM // 2)], 0)
            )
        product = jnp.dot(matrix, jnp.concatenate(sides, 1), preferred_element_type=F32)
        product = product[0 : 2 * CHUNK] + product[2 * CHUNK :]
        even, odd = product[:CHUNK], product[CHUNK:]
        stay = jnp.where(low, even[:, :LANES], odd[:, LANES:])
        cross = jnp.where(low, even[:, LANES:], odd[:, :LANES])
        chunks.append(stay + swap(cross))
    value = jnp.concatenate(chunks, 0)
    low = low_lanes((HALF, LANES))
    zero = jnp.zeros((HALF, LANES), F32)
    other = swap(value)
    operand = jnp.concatenate(
        [
            jnp.where(low, value, zero).astype(BF16),
            jnp.where(low, other, zero).astype(BF16),
            jnp.where(low, zero, other).astype(BF16),
            jnp.where(low, zero, value).astype(BF16),
        ],
        0,
    )
    copies[3].wait()
    s_ref[...] = jnp.dot(table_ref[...], operand, preferred_element_type=F32)
    tail = swap(value[LSEG - HALF : LSEG - HALF + SUB])
    high_part = tail.astype(BF16).astype(F32)
    tail = jnp.where(low_lanes((SUB, LANES)), high_part, swap(tail - high_part))
    copies[2].wait()
    valid = valid_ref[...].astype(F32)
    valid = jnp.broadcast_to(jnp.concatenate([valid, valid], 1), (SUB, LANES))
    extra = jnp.concatenate([tail, valid], 0).astype(BF16)
    count = NF // segs
    width = window(count)
    for d in range(n_win):
        for e in range(n_bin):
            chunk = lax.rem(my_win + d, n_win) * n_bin + lax.rem(my_bin + e, n_bin)
            start = pl.multiple_of(window_start(chunk, count), SUB)
            out_ref = outs[d * n_bin + e]
            out_ref[0:16, :] = extra
            out_ref[16:, :] = s_ref[pl.ds(start, width), :].astype(BF16)
    copies[4].wait()


def whiten_kernel(sizes, *refs):
    n_win, n_bin = sizes
    segs = n_win * n_bin
    parts, (windows_ref, out_ref, s_ref) = refs[:segs], refs[segs:]
    my_win, my_bin = lax.axis_index("win"), lax.axis_index("bin")
    count = NF // segs
    width = window(count)
    chunk = my_win * n_bin + my_bin
    extras = [part[0:16, :].astype(F32) for part in parts]
    tails = []
    for d in range(n_win):
        for e in range(n_bin):
            win = lax.rem(my_win - d + n_win, n_win)
            core = lax.rem(my_bin - e + n_bin, n_bin)
            after = (e + 1) % n_bin
            first = core == 0
            use_same = jnp.where(first, 0.0, 1.0).astype(F32)
            use_other = jnp.where(jnp.logical_and(first, win != 0), 1.0, 0.0).astype(F32)
            same = extras[d * n_bin + after][0:SUB]
            other = extras[(d + 1) % n_win * n_bin + after][0:SUB]
            tails.append(jnp.concatenate(spread(same * use_same + other * use_other), 0).astype(BF16))
    spectra = jnp.dot(windows_ref[0:width, 0 : 4 * SUB], jnp.concatenate(tails, 1), preferred_element_type=F32)
    spectra = spectra + jnp.concatenate([part[16:, :].astype(F32) for part in parts], 1)
    s_ref[...] = spectra
    square = spectra * spectra
    square_high = square.astype(BF16)
    square_low = (square - square_high.astype(F32)).astype(BF16)
    smooth = windows_ref[width:, 0:width]
    energy = jnp.dot(smooth, square_high, preferred_element_type=F32) + jnp.dot(
        smooth, square_low, preferred_element_type=F32
    )
    own = pl.multiple_of(chunk * count - window_start(chunk, count), SUB)
    whites = []
    for s in range(segs):
        at = slice(s * LANES, (s + 1) * LANES)
        total = energy[:, at] + swap(energy[:, at])
        scale = extras[s][SUB : SUB + 1] * lax.rsqrt(total * (1.0 / (2.0 * SMOOTH)) + EPSILON)
        whites.append(s_ref[pl.ds(own, count), at] * scale)
    for g in range(count // SUB):
        tiles = [white[SUB * g : SUB * g + SUB] for white in whites]
        out_ref[SUB * segs * g : SUB * segs * (g + 1), :] = jnp.concatenate(tiles, 0).astype(BF16)


def operands(values):
    left, right = [], []
    for s in range(values.shape[0] // SUB):
        real_even, real_odd, imag_even, imag_odd = spread(values[SUB * s : SUB * s + SUB])
        left += [real_even, real_odd, imag_even, imag_odd]
        right += [-imag_even, -imag_odd, real_even, real_odd]
    return jnp.concatenate(left, 0), jnp.concatenate(right, 0)


def home_kernel(home_ref, out_ref):
    groups, rows, depth = out_ref.shape
    row = lax.broadcasted_iota(jnp.int32, (rows, LANES), 0)
    lane = lax.broadcasted_iota(jnp.int32, (rows, LANES), 1)
    pick = jnp.where(lane % SB == 2 * (row // SUB) + lane // SB, 1.0, 0.0).astype(BF16)
    row = lax.broadcasted_iota(jnp.int32, (rows, depth), 0)
    lane = lax.broadcasted_iota(jnp.int32, (rows, depth), 1)
    diagonal = row % SUB == lane % SUB
    size = home_ref.shape[0] // groups
    for g in range(groups):
        left, _ = operands(home_ref[size * g : size * (g + 1), :].astype(F32))
        turned = lax.dot_general(pick, left.astype(BF16), (((1,), (1,)), ((), ())), preferred_element_type=F32)
        out_ref[g] = jnp.where(diagonal, turned, 0.0).astype(BF16)


def cross_kernel(offset, factor, home_ref, away_ref, *refs):
    out_hbm, out_ref, sem = refs[-3:]
    groups = home_ref.shape[0]
    size = away_ref.shape[0] // groups
    copies = []
    for g in range(groups):
        block = jnp.concatenate(operands(away_ref[size * g : size * (g + 1), :].astype(F32)), 1).astype(BF16)
        product = jnp.dot(home_ref[g], block, preferred_element_type=F32) * factor
        at = pl.ds(SUB * g, SUB)
        for c in range(2):
            for t in range(SB // 2):
                out_ref[c, SUB * g : SUB * g + SUB, t * LANES : (t + 1) * LANES] = product[
                    SUB * t : SUB * t + SUB, c * LANES : (c + 1) * LANES
                ]
            copies.append(pltpu.make_async_copy(out_ref.at[c, at], out_hbm.at[offset, 0, c, at], sem.at[2 * g + c]))
            copies[-1].start()
    for copy in copies:
        copy.wait()


def shifted(value, axis, steps):
    size = lax.axis_size(axis)
    return lax.ppermute(value, axis, [(i, (i + steps) % size) for i in range(size)])


def cost(flops, moved):
    return pl.CostEstimate(flops=int(flops), bytes_accessed=int(moved), transcendentals=0)


def room(limit):
    return pltpu.CompilerParams(vmem_limit_bytes=limit)


VMEM = pl.BlockSpec(memory_space=pltpu.VMEM)
HBM = pl.BlockSpec(memory_space=pl.ANY)


def per_device(raw_counts, seg_valid):
    n_win, n_bin = lax.axis_size("win"), lax.axis_size("bin")
    segs = n_win * n_bin
    samples = raw_counts[:, 0, :]
    rows = samples.shape[0]
    assert rows == LSEG and NF % (SUB * segs) == 0
    bins = NF // segs
    groups = bins // SUB
    rows_sent = window(bins) + 16
    matrix, table, windows = (jnp.asarray(t) for t in (tap_matrix(), transform_table(), window_tables(segs)))
    *sent, own_window = pl.pallas_call(
        functools.partial(segment_kernel, (n_win, n_bin)),
        out_shape=(jax.ShapeDtypeStruct((rows_sent, LANES), BF16),) * segs
        + (jax.ShapeDtypeStruct(windows.shape[1:], BF16),),
        in_specs=[pl.BlockSpec(memory_space=pltpu.HBM)] * 5,
        out_specs=(VMEM,) * (segs + 1),
        scratch_shapes=[
            pltpu.VMEM((BACK + 2 * HALF, samples.shape[1]), BF16),
            pltpu.VMEM(matrix.shape, BF16),
            pltpu.VMEM(seg_valid.shape, jnp.int32),
            pltpu.VMEM(table.shape, BF16),
            pltpu.VMEM((NF, LANES), F32),
            pltpu.SemaphoreType.DMA((5,)),
        ],
        cost_estimate=cost(8 * samples.size * 2 * LANES, 2 * (samples.size + table.size)),
        compiler_params=room(16 << 20),
        name="segment",
    )(*(pltpu.with_memory_space_constraint(v, pltpu.HBM) for v in (samples, matrix, seg_valid, table, windows)))

    parts = [sent[0]] + [None] * (segs - 1)
    for d in reversed(range(n_win)):
        for e in range(n_bin):
            if d or e:
                route = [
                    (w * n_bin + c, (w + d) % n_win * n_bin + (c + e) % n_bin) for w in range(n_win) for c in range(n_bin)
                ]
                parts[d * n_bin + e] = lax.ppermute(sent[d * n_bin + e], ("win", "bin"), route)
    home = pl.pallas_call(
        functools.partial(whiten_kernel, (n_win, n_bin)),
        out_shape=jax.ShapeDtypeStruct((segs * bins, LANES), BF16),
        in_specs=[VMEM] * (segs + 1),
        out_specs=VMEM,
        scratch_shapes=[pltpu.VMEM((window(bins), segs * LANES), F32)],
        cost_estimate=cost(4 * bins * window(bins) * segs * LANES, 8 * segs * bins * LANES),
        compiler_params=room(6 << 20),
        name="whiten",
    )(*parts, own_window)

    aways = [shifted(home, "blk", offset) for offset in range(1, ROUNDS + 1)]
    depth = segs * 4 * SUB
    tall = SB // 2 * SUB
    turned = pl.pallas_call(
        home_kernel,
        out_shape=jax.ShapeDtypeStruct((groups, tall, depth), BF16),
        in_specs=[VMEM],
        out_specs=VMEM,
        cost_estimate=cost(2 * groups * tall * depth * LANES, 2 * groups * tall * depth),
        compiler_params=room(6 << 20),
        name="home",
    )(home)

    stacks = None
    for offset in range(ROUNDS):
        extra = [] if stacks is None else [stacks]
        stacks = pl.pallas_call(
            functools.partial(cross_kernel, offset, 1.0 / segs),
            out_shape=jax.ShapeDtypeStruct((ROUNDS, 1, 2, bins, SB * SB), F32),
            in_specs=[VMEM] * 2 + [HBM] * len(extra),
            out_specs=HBM,
            scratch_shapes=[pltpu.VMEM((2, bins, SB * SB), F32), pltpu.SemaphoreType.DMA((2 * groups,))],
            input_output_aliases={2: 0} if extra else {},
            cost_estimate=cost(4 * groups * tall * depth * LANES, 8 * bins * SB * SB),
            compiler_params=room(8 << 20),
            name="cross",
        )(turned, aways[offset], *extra)
    return stacks


def solution(mesh):
    in_specs = (P(("win", "bin"), ("parts", "blk"), None), P(("win", "bin"), ("parts", "blk")))
    out_specs = P(None, ("parts", "blk"), None, ("win", "bin"), None)
    return jax.shard_map(
        per_device, mesh=mesh, in_specs=in_specs, out_specs=out_specs, check_vma=False
    )
```

time: 22.4 us -> 21.1 us (0.942)
  Pallas kernels: 7.42 us -> 6.9 us
  waiting for transfers between devices: 7.07 us -> 6.68 us
  starting transfers between devices: 7.76 us -> 7.37 us
    ppermute x5 -> x2, waiting for transfers between devices: 7.07 us -> 3.36 us  [shifted(): lax.ppermute(value, axis, [(i, (i + steps) % size) for i in range(size)])]
    ppermute x5 -> x2, starting transfers between devices: 7.76 us -> 4.22 us  [shifted(): lax.ppermute(value, axis, [(i, (i + steps) % size) for i in range(size)])]
    ppermute x0 -> x3, waiting for transfers between devices: none -> 3.32 us  [per_device(): lax.ppermute(sent[d * n_bin + e], ('win', 'bin'), route)]
    ppermute x0 -> x3, starting transfers between devices: none -> 3.15 us  [per_device(): lax.ppermute(sent[d * n_bin + e], ('win', 'bin'), route)]
    pallas_call x1, Pallas kernels: 2.48 us -> 2.11 us  [per_device(): pl.pallas_call(functools.partial(segment_kernel, (n_win, n_bin)), out_sha...]
  transfers between devices with their start and end apart: 5 -> 5, of which waited for: 4 -> 4; matrix products, arithmetic and copies ran while one was open for 0% -> 0% of each run, Pallas kernels for 10% -> 11%
where the time goes in v3:
time: 21.1 us; the launch traced here: 21 us
  starting transfers between devices  7.37 us (35%)
  Pallas kernels  6.9 us (33%)
  waiting for transfers between devices  6.68 us (32%)
    ppermute x2, starting transfers between devices, shifted(): lax.ppermute(value, axis, [(i, (i + steps) % size) for i in range(size)])  4.22 us
    pallas_call x2, Pallas kernels, per_device(): pl.pallas_call(functools.partial(cross_kernel, offset, 1.0 / segs), out_s...  3.87 us
    ppermute x2, waiting for transfers between devices, shifted(): lax.ppermute(value, axis, [(i, (i + steps) % size) for i in range(size)])  3.36 us
    ppermute x3, waiting for transfers between devices, per_device(): lax.ppermute(sent[d * n_bin + e], ('win', 'bin'), route)  3.32 us
    ppermute x3, starting transfers between devices, per_device(): lax.ppermute(sent[d * n_bin + e], ('win', 'bin'), route)  3.15 us
    pallas_call x1, Pallas kernels, per_device(): pl.pallas_call(functools.partial(segment_kernel, (n_win, n_bin)), out_sha...  2.11 us
    pallas_call x1, Pallas kernels, per_device(): pl.pallas_call(functools.partial(whiten_kernel, (n_win, n_bin)), out_shap...  0.53 us
  transfers between devices with their start and end apart: 5, of which 4 were waited for; matrix products, arithmetic and copies ran while one was open for 0% of the time, Pallas kernels for 11%

profile of v3, /device:TPU:0, one launch (start us, length us, event | category | flops | bytes accessed | tf_op | source)
XLA Modules:
  0.0 21.0 jit_solution(12872420812582040558)
XLA Ops:
  0.0 2.1 %segment.1 = (bf16[128,128]{1,0:T(8,128)(2,1)S(1)}, bf16[128,128]{1,0:T(8,128)(2,1)S(1)}, bf16[128,128]{1,0:T(8,128)(2,1)S(1)}, bf16[128,128]{1,0:T(8,128)(2,1)S(1)}, bf16[192,128]{1,0:T(8,128)(2,1)S(1)}) custom-call(bf16[600,640]{1,0:T(8,128)(2,1)} %bitcast.1, bf16[128,240]{1,0:T(8,128)(2,1)} %constant.6.clone.taps_hbm, s32[1,64]{1,0:T(1,128)} %valid_hbm.1, ...), custom_call_target="tpu_custom_call" | custom-call | flops 786432000 | bytes 1587200 | tf_op jit(solution)/shard_map/segment/pallas_call | solution.py:303
  2.1 0.6 %collective-permute-start = (bf16[128,128]{1,0:T(8,128)(2,1)S(1)}, bf16[128,128]{1,0:T(8,128)(2,1)S(1)}, u32[]{:S(2)}, u32[]{:S(2)}) collective-permute-start(bf16[128,128]{1,0:T(8,128)(2,1)S(1)} %get-tuple-element.11), channel_id=1, source_target_pairs={{0,1},{1,0},{2,3},{3,2},{4,5},{5,4},{6,7},{7,6},{8,9},{9,8},{10,11... | collective-permute-start | bytes 98312 | tf_op jit(solution)/shard_map/ppermute | solution.py:329
  2.7 2.6 %collective-permute-start.1 = (bf16[128,128]{1,0:T(8,128)(2,1)S(1)}, bf16[128,128]{1,0:T(8,128)(2,1)S(1)}, u32[]{:S(2)}, u32[]{:S(2)}) collective-permute-start(bf16[128,128]{1,0:T(8,128)(2,1)S(1)} %get-tuple-element.12), channel_id=1, source_target_pairs={{0,2},{1,3},{2,0},{3,1},{4,6},{5,7},{6,4},{7,5},{8,10},{9,11},{10,... | collective-permute-start | bytes 98312 | tf_op jit(solution)/shard_map/ppermute | solution.py:329
  5.2 0.0 collective-permute-start.2
  5.3 0.0 collective-permute-done.refs_1_
  5.3 1.9 %collective-permute-done.1.refs_2_ = bf16[128,128]{1,0:T(8,128)(2,1)S(1)} collective-permute-done((bf16[128,128]{1,0:T(8,128)(2,1)S(1)}, bf16[128,128]{1,0:T(8,128)(2,1)S(1)}, u32[]{:S(2)}, u32[]{:S(2)}) %collective-permute-start.1) | collective-permute-done | bytes 32800 | tf_op jit(solution)/shard_map/ppermute | solution.py:329
  7.2 1.4 %collective-permute-done.2.refs_3_ = bf16[128,128]{1,0:T(8,128)(2,1)S(1)} collective-permute-done((bf16[128,128]{1,0:T(8,128)(2,1)S(1)}, bf16[128,128]{1,0:T(8,128)(2,1)S(1)}, u32[]{:S(2)}, u32[]{:S(2)}) %collective-permute-start.2) | collective-permute-done | bytes 32800 | tf_op jit(solution)/shard_map/ppermute | solution.py:329
  8.6 0.5 %whiten.1.home_ref = bf16[320,128]{1,0:T(8,128)(2,1)S(1)} custom-call(bf16[128,128]{1,0:T(8,128)(2,1)S(1)} %get-tuple-element.10.refs_0_, bf16[128,128]{1,0:T(8,128)(2,1)S(1)} %collective-permute-done.refs_1_, bf16[128,128]{1,0:T(8,128)(2,1)S(1)} %collective-permute-done.1.refs_2_, bf16[128,128]{1,0:T(8,128)(2,1)S(1)} %collective-permute-done.2.refs_3_, ...), custom_call_target="tpu_custom_call" | custom-call | flops 18350080 | bytes 327680 | tf_op jit(solution)/shard_map/whiten/pallas_call | solution.py:330
  9.1 1.6 %collective-permute-start.4 = (bf16[320,128]{1,0:T(8,128)(2,1)S(1)}, bf16[320,128]{1,0:T(8,128)(2,1)S(1)}, u32[]{:S(2)}, u32[]{:S(2)}) collective-permute-start(bf16[320,128]{1,0:T(8,128)(2,1)S(1)} %whiten.1.home_ref), channel_id=1, source_target_pairs={{0,4},{4,8},{8,12},{12,0},{1,5},{5,9},{9,13},{13,1},{2,6},{6,10},{... | collective-permute-start | bytes 245768 | tf_op jit(solution)/shard_map/ppermute | solution.py:278
  10.8 2.6 %collective-permute-start.3 = (bf16[320,128]{1,0:T(8,128)(2,1)S(1)}, bf16[320,128]{1,0:T(8,128)(2,1)S(1)}, u32[]{:S(2)}, u32[]{:S(2)}) collective-permute-start(bf16[320,128]{1,0:T(8,128)(2,1)S(1)} %whiten.1.home_ref), channel_id=1, source_target_pairs={{0,8},{4,12},{8,0},{12,4},{1,9},{5,13},{9,1},{13,5},{2,10},{6,14},... | collective-permute-start | bytes 245768 | tf_op jit(solution)/shard_map/ppermute | solution.py:278
  13.3 0.4 %home.1.home_ref = bf16[10,256,128]{2,1,0:T(8,128)(2,1)S(1)} custom-call(bf16[320,128]{1,0:T(8,128)(2,1)S(1)} %whiten.1.home_ref), custom_call_target="tpu_custom_call" | custom-call | flops 83886080 | bytes 655360 | tf_op jit(solution)/shard_map/home/pallas_call | solution.py:344
  13.8 2.3 %collective-permute-done.4.away_ref = bf16[320,128]{1,0:T(8,128)(2,1)S(1)} collective-permute-done((bf16[320,128]{1,0:T(8,128)(2,1)S(1)}, bf16[320,128]{1,0:T(8,128)(2,1)S(1)}, u32[]{:S(2)}, u32[]{:S(2)}) %collective-permute-start.4) | collective-permute-done | bytes 81952 | tf_op jit(solution)/shard_map/ppermute | solution.py:278
  16.1 1.9 %cross.2.refs_0_ = f32[2,1,2,80,4096]{4,3,2,1,0:T(8,128)} custom-call(bf16[10,256,128]{2,1,0:T(8,128)(2,1)S(1)} %home.1.home_ref, bf16[320,128]{1,0:T(8,128)(2,1)S(1)} %collective-permute-done.4.away_ref), custom_call_target="tpu_custom_call" | custom-call | flops 167772160 | bytes 2621440 | tf_op jit(solution)/shard_map/cross/pallas_call | solution.py:357
  18.0 1.1 %collective-permute-done.3.away_ref = bf16[320,128]{1,0:T(8,128)(2,1)S(1)} collective-permute-done((bf16[320,128]{1,0:T(8,128)(2,1)S(1)}, bf16[320,128]{1,0:T(8,128)(2,1)S(1)}, u32[]{:S(2)}, u32[]{:S(2)}) %collective-permute-start.3) | collective-permute-done | bytes 81952 | tf_op jit(solution)/shard_map/ppermute | solution.py:278
  19.1 1.9 %cross.3 = f32[2,1,2,80,4096]{4,3,2,1,0:T(8,128)} custom-call(bf16[10,256,128]{2,1,0:T(8,128)(2,1)S(1)} %home.1.home_ref, bf16[320,128]{1,0:T(8,128)(2,1)S(1)} %collective-permute-done.3.away_ref, f32[2,1,2,80,4096]{4,3,2,1,0:T(8,128)} %cross.2.refs_0_), custom_call_target="tpu_custom_call", output_to_operand_aliasing={{}: (2, {})} | custom-call | flops 167772160 | bytes 2621440 | tf_op jit(solution)/shard_map/cross/pallas_call | solution.py:357
Async XLA Ops:
  2.1 3.2 %collective-permute-start = (bf16[128,128]{1,0:T(8,128)(2,1)S(1)}, bf16[128,128]{1,0:T(8,128)(2,1)S(1)}, u32[]{:S(2)}, u32[]{:S(2)}) collective-permute-start(bf16[128,128]{1,0:T(8,128)(2,1)S(1)} %get-tuple-element.11), channel_id=1, source_target_pairs={{0,1},{1,0},{2,3},{3,2},{4,5},{5,4},{6,7},{7,6},{8,9},{9,8},{10,11... | collective-permute-start | bytes 98312 | tf_op jit(solution)/shard_map/ppermute | solution.py:329
  2.7 4.5 %collective-permute-start.1 = (bf16[128,128]{1,0:T(8,128)(2,1)S(1)}, bf16[128,128]{1,0:T(8,128)(2,1)S(1)}, u32[]{:S(2)}, u32[]{:S(2)}) collective-permute-start(bf16[128,128]{1,0:T(8,128)(2,1)S(1)} %get-tuple-element.12), channel_id=1, source_target_pairs={{0,2},{1,3},{2,0},{3,1},{4,6},{5,7},{6,4},{7,5},{8,10},{9,11},{10,... | collective-permute-start | bytes 98312 | tf_op jit(solution)/shard_map/ppermute | solution.py:329
  5.2 3.4 %collective-permute-start.2 = (bf16[128,128]{1,0:T(8,128)(2,1)S(1)}, bf16[128,128]{1,0:T(8,128)(2,1)S(1)}, u32[]{:S(2)}, u32[]{:S(2)}) collective-permute-start(bf16[128,128]{1,0:T(8,128)(2,1)S(1)} %get-tuple-element.13), channel_id=1, source_target_pairs={{0,3},{1,2},{2,1},{3,0},{4,7},{5,6},{6,5},{7,4},{8,11},{9,10},{10,... | collective-permute-start | bytes 98312 | tf_op jit(solution)/shard_map/ppermute | solution.py:329
  9.1 6.9 %collective-permute-start.4 = (bf16[320,128]{1,0:T(8,128)(2,1)S(1)}, bf16[320,128]{1,0:T(8,128)(2,1)S(1)}, u32[]{:S(2)}, u32[]{:S(2)}) collective-permute-start(bf16[320,128]{1,0:T(8,128)(2,1)S(1)} %whiten.1.home_ref), channel_id=1, source_target_pairs={{0,4},{4,8},{8,12},{12,0},{1,5},{5,9},{9,13},{13,1},{2,6},{6,10},{... | collective-permute-start | bytes 245768 | tf_op jit(solution)/shard_map/ppermute | solution.py:278
  10.8 8.3 %collective-permute-start.3 = (bf16[320,128]{1,0:T(8,128)(2,1)S(1)}, bf16[320,128]{1,0:T(8,128)(2,1)S(1)}, u32[]{:S(2)}, u32[]{:S(2)}) collective-permute-start(bf16[320,128]{1,0:T(8,128)(2,1)S(1)} %whiten.1.home_ref), channel_id=1, source_target_pairs={{0,8},{4,12},{8,0},{12,4},{1,9},{5,13},{9,1},{13,5},{2,10},{6,14},... | collective-permute-start | bytes 245768 | tf_op jit(solution)/shard_map/ppermute | solution.py:278
